TPU v7x, 32 devices: a whole 2x2x4 slice. The times are simulated.
32 devices in a mesh: seq: 8 (over z, y), fsdp: 4 (over x, core).
Axes of the slice: x: 2, y: 2, z: 4, core: 2. Of those that a mesh axis runs over, the one named last changes fastest.
Arguments:
- tokens: bfloat16 [4, 1024, 768], P('fsdp', 'seq')
- lengths: int32 [4], P('fsdp'), may hold values from 341 to 1024
- block_order: int32 [8], replicated, may hold values from 0 to 7, each once
- qkv_weight: bfloat16 [768, 2304], P('fsdp'), may hold values from -0.21875 to 0.21875
- q_bias: bfloat16 [768], P('fsdp'), may hold values from -3 to 3
- v_bias: bfloat16 [768], P('fsdp'), may hold values from -0.119628906 to 0.119628906
- out_weight: bfloat16 [768, 768], P('fsdp'), may hold values from -6 to 6
- out_bias: bfloat16 [768], P('fsdp'), may hold values from -3 to 3
- norm1_gain: bfloat16 [768], P('fsdp'), may hold values from 0.5 to 1.5
- norm1_shift: bfloat16 [768], P('fsdp'), may hold values from -3 to 3
- up_weight: bfloat16 [768, 3072], P('fsdp'), may hold values from -0.21875 to 0.21875
- up_bias: bfloat16 [3072], P('fsdp'), may hold values from -3 to 3
- down_weight: bfloat16 [3072, 768], P('fsdp'), may hold values from -0.109375 to 0.109375
- down_bias: bfloat16 [768], P('fsdp'), may hold values from -3 to 3
- norm2_gain: bfloat16 [768], P('fsdp'), may hold values from 0.5 to 1.5
- norm2_shift: bfloat16 [768], P('fsdp'), may hold values from -3 to 3
- cotangent: bfloat16 [4, 1024, 768], P('fsdp', 'seq'), may hold values from -6 to 6
Outputs:
- encoded: bfloat16 [4, 1024, 768], P('fsdp', 'seq')
- input_grad: float32 [4, 1024, 768], P('fsdp', 'seq')
- qkv_grad: float32 [768, 2304], P('fsdp')
- q_bias_grad: float32 [768], P('fsdp')
- v_bias_grad: float32 [768], P('fsdp')
- out_weight_grad: float32 [768, 768], P('fsdp')
- out_bias_grad: float32 [768], P('fsdp')
- norm1_gain_grad: float32 [768], P('fsdp')
- norm1_shift_grad: float32 [768], P('fsdp')
- up_weight_grad: float32 [768, 3072], P('fsdp')
- up_bias_grad: float32 [3072], P('fsdp')
- down_weight_grad: float32 [3072, 768], P('fsdp')
- down_bias_grad: float32 [768], P('fsdp')
- norm2_gain_grad: float32 [768], P('fsdp')
- norm2_shift_grad: float32 [768], P('fsdp')
Inputs may be any that keep to these rules, and one draw needn't show every extreme that they name: Rows j * 128 to (j + 1) * 128 - 1 of each sequence in tokens and cotangent hold the positions block_order[j] * 128 onward; each block number appears once. The first lengths[s] positions of sequence s are real tokens; only they serve as keys.
All inputs are finite; a program needn't handle non-finite values.
Results may differ from a plain program's by a relative error of at most 0.018.
The roundings to bfloat16 on the way count: a program that leaves them out, or rounds other values in their place, can miss the bound.
Values may be sent and summed in bfloat16 or wider, within the bound.
No kernel may reach another device: no remote copies, remote signals or barrier semaphores. Data moves between devices by JAX's collectives and lax.ppermute only.
A program may use at most 192 MiB of HBM per device.

v0:
```python
import jax
import jax.numpy as jnp
from jax import lax
from jax.sharding import PartitionSpec as P

HEADS = 12


epsilon = 1e-06
masked_out = -1e30


def positions(block_order, block_len):
    offsets = jnp.arange(block_len, dtype=jnp.int32)
    return (block_order[:, None] * block_len + offsets[None, :]).reshape(-1)


def norm_forward(hidden, gain, shift):
    centre = hidden - jnp.mean(hidden, axis=-1, keepdims=True)
    spread = lax.rsqrt(jnp.mean(centre * centre, axis=-1, keepdims=True) + epsilon)
    normed = centre * spread
    return (normed * gain + shift, normed, spread)


def norm_backward(upstream, normed, spread, gain):
    scaled = upstream * gain
    grad_in = spread * (
        scaled
        - jnp.mean(scaled, axis=-1, keepdims=True)
        - normed * jnp.mean(scaled * normed, axis=-1, keepdims=True)
    )
    return (grad_in, jnp.sum(upstream * normed, axis=0), jnp.sum(upstream, axis=0))


def gelu_exact(pre):
    return 0.5 * pre * (1.0 + lax.erf(pre * 0.7071067811865476))


def gelu_slope(pre):
    return (
        0.5 * (1.0 + lax.erf(pre * 0.7071067811865476))
        + pre * jnp.exp(-0.5 * pre * pre) * 0.3989422804014327
    )


def body(
    tokens,
    lengths,
    block_order,
    qkv_weight,
    q_bias,
    v_bias,
    out_weight,
    out_bias,
    norm1_gain,
    norm1_shift,
    up_weight,
    up_bias,
    down_weight,
    down_bias,
    norm2_gain,
    norm2_shift,
    cotangent,
):
    seq_local, block_len, model_width = tokens.shape
    seq_count = lax.axis_size("seq")
    full_len = block_len * seq_count
    row_count = seq_local * block_len
    head_count = HEADS
    head_size = model_width // head_count
    score_scale = head_size ** (-0.5)
    grad_scale = (row_count * seq_count * lax.axis_size("fsdp")) ** (-0.5)
    head_shape = (seq_local, block_len, head_count, head_size)
    flat_shape = (seq_local, block_len, model_width)
    gathered = (
        lax.all_gather(qkv_weight, "fsdp", axis=0, tiled=True),
        lax.all_gather(out_weight, "fsdp", axis=0, tiled=True),
        lax.all_gather(up_weight, "fsdp", axis=0, tiled=True),
        lax.all_gather(down_weight, "fsdp", axis=0, tiled=True),
        lax.all_gather(q_bias, "fsdp", axis=0, tiled=True),
        lax.all_gather(v_bias, "fsdp", axis=0, tiled=True),
        lax.all_gather(out_bias, "fsdp", axis=0, tiled=True),
        lax.all_gather(norm1_gain, "fsdp", axis=0, tiled=True),
        lax.all_gather(norm1_shift, "fsdp", axis=0, tiled=True),
        lax.all_gather(up_bias, "fsdp", axis=0, tiled=True),
        lax.all_gather(down_bias, "fsdp", axis=0, tiled=True),
        lax.all_gather(norm2_gain, "fsdp", axis=0, tiled=True),
        lax.all_gather(norm2_shift, "fsdp", axis=0, tiled=True),
    )
    qkv_full, out_full, up_full, down_full = (gathered[0], gathered[1], gathered[2], gathered[3])
    smalls = [item.astype(jnp.float32) for item in gathered[4:]]
    bias_q, bias_v, bias_out, gain_one, shift_one, bias_up, bias_down, gain_two, shift_two = smalls
    flat_in = tokens.reshape(row_count, model_width)
    projected = jnp.dot(flat_in, qkv_full, preferred_element_type=jnp.float32)
    queries_flat = (projected[:, :model_width] + bias_q).astype(jnp.bfloat16).reshape(flat_shape)
    keys_own = projected[:, model_width : 2 * model_width].astype(jnp.bfloat16).reshape(flat_shape)
    values_own = (projected[:, 2 * model_width :] + bias_v).astype(jnp.bfloat16).reshape(flat_shape)
    queries = queries_flat.reshape(head_shape)
    keys_all, values_all = (
        lax.all_gather(keys_own, "seq", axis=1, tiled=True),
        lax.all_gather(values_own, "seq", axis=1, tiled=True),
    )
    valid = positions(block_order, block_len)[None, :] < lengths[:, None]
    key_block = min(512, full_len)
    key_steps = full_len // key_block
    slice_shape = (seq_local, key_block, head_count, head_size)

    def logits_for(query_rows, key_rows, mask_rows):
        logits = (
            jnp.einsum("sqhd,skhd->shqk", query_rows, key_rows, preferred_element_type=jnp.float32)
            * score_scale
        )
        return jnp.where(mask_rows[:, None, None, :], logits, masked_out)

    def key_slices(step):
        start = step * key_block
        key_rows = lax.dynamic_slice_in_dim(keys_all, start, key_block, 1).reshape(slice_shape)
        value_rows = lax.dynamic_slice_in_dim(values_all, start, key_block, 1).reshape(slice_shape)
        mask_rows = lax.dynamic_slice_in_dim(valid, start, key_block, 1)
        return (key_rows, value_rows, mask_rows)

    def stat_step(step, carry):
        running, total = carry
        key_rows, value_rows, mask_rows = key_slices(step)
        logits = logits_for(queries, key_rows, mask_rows)
        highest = jnp.maximum(running, jnp.max(logits, axis=-1))
        terms = jnp.where(mask_rows[:, None, None, :], jnp.exp(logits - highest[..., None]), 0.0)
        return (highest, total * jnp.exp(running - highest) + jnp.sum(terms, axis=-1))

    stat_shape = (seq_local, head_count, block_len)
    running, total = lax.fori_loop(
        0,
        key_steps,
        stat_step,
        (jnp.full(stat_shape, masked_out, jnp.float32), jnp.zeros(stat_shape, jnp.float32)),
    )
    log_total = running + jnp.log(total)

    def context_step(step, context):
        key_rows, value_rows, mask_rows = key_slices(step)
        logits = logits_for(queries, key_rows, mask_rows)
        weights_blk = jnp.where(
            mask_rows[:, None, None, :], jnp.exp(logits - log_total[..., None]), 0.0
        ).astype(jnp.bfloat16)
        return context + jnp.einsum(
            "shqk,skhd->sqhd", weights_blk, value_rows, preferred_element_type=jnp.float32
        )

    context = lax.fori_loop(0, key_steps, context_step, jnp.zeros(head_shape, jnp.float32)).astype(
        jnp.bfloat16
    )
    context_flat = context.reshape(row_count, model_width)
    attended = jnp.dot(context_flat, out_full, preferred_element_type=jnp.float32) + bias_out
    first_sum = flat_in.astype(jnp.float32) + attended
    first_out, first_norm, first_spread = norm_forward(first_sum, gain_one, shift_one)
    first_bf = first_out.astype(jnp.bfloat16)
    pre_act = jnp.dot(first_bf, up_full, preferred_element_type=jnp.float32) + bias_up
    activated = gelu_exact(pre_act).astype(jnp.bfloat16)
    second_sum = (
        first_out + jnp.dot(activated, down_full, preferred_element_type=jnp.float32) + bias_down
    )
    second_out, second_norm, second_spread = norm_forward(second_sum, gain_two, shift_two)
    encoded = second_out.astype(jnp.bfloat16).reshape(flat_shape)
    regathered = (
        lax.all_gather(qkv_weight, "fsdp", axis=0, tiled=True),
        lax.all_gather(out_weight, "fsdp", axis=0, tiled=True),
        lax.all_gather(up_weight, "fsdp", axis=0, tiled=True),
        lax.all_gather(down_weight, "fsdp", axis=0, tiled=True),
    )
    qkv_back, out_back, up_back, down_back = (
        regathered[0],
        regathered[1],
        regathered[2],
        regathered[3],
    )
    upstream = cotangent.reshape(row_count, model_width).astype(jnp.float32)
    grad_second, grad_gain_two, grad_shift_two = norm_backward(
        upstream, second_norm, second_spread, gain_two
    )
    grad_second_bf = grad_second.astype(jnp.bfloat16)
    grad_down = jnp.einsum(
        "nf,nd->fd", activated, grad_second_bf, preferred_element_type=jnp.float32
    )
    grad_act = jnp.einsum(
        "nd,fd->nf", grad_second_bf, down_back, preferred_element_type=jnp.float32
    )
    grad_pre = grad_act * gelu_slope(pre_act)
    grad_pre_bf = grad_pre.astype(jnp.bfloat16)
    grad_up = jnp.einsum("nd,nf->df", first_bf, grad_pre_bf, preferred_element_type=jnp.float32)
    grad_first_out = grad_second + jnp.einsum(
        "nf,df->nd", grad_pre_bf, up_back, preferred_element_type=jnp.float32
    )
    grad_first, grad_gain_one, grad_shift_one = norm_backward(
        grad_first_out, first_norm, first_spread, gain_one
    )
    grad_first_bf = grad_first.astype(jnp.bfloat16)
    grad_out = jnp.einsum(
        "nc,nd->cd", context_flat, grad_first_bf, preferred_element_type=jnp.float32
    )
    grad_context_flat = (
        jnp.einsum("nd,cd->nc", grad_first_bf, out_back, preferred_element_type=jnp.float32)
        .astype(jnp.bfloat16)
        .reshape(flat_shape)
    )
    grad_context = grad_context_flat.reshape(head_shape)
    correction = jnp.einsum(
        "sqhd,sqhd->shq", grad_context.astype(jnp.float32), context.astype(jnp.float32)
    )

    def mixed_terms(logits, mask_rows, lse_rows, corr_rows, grad_rows, value_rows):
        probs = jnp.where(mask_rows[:, None, None, :], jnp.exp(logits - lse_rows[..., None]), 0.0)
        grad_logit = jnp.einsum(
            "sqhd,skhd->shqk", grad_rows, value_rows, preferred_element_type=jnp.float32
        )
        mixed = (probs * (grad_logit - corr_rows[..., None])).astype(jnp.bfloat16)
        return (probs.astype(jnp.bfloat16), mixed)

    def partial_step(step, carry):
        grad_query, grad_keys, grad_values = carry
        key_rows, value_rows, mask_rows = key_slices(step)
        logits = logits_for(queries, key_rows, mask_rows)
        probs_bf, mixed = mixed_terms(
            logits, mask_rows, log_total, correction, grad_context, value_rows
        )
        grad_query = (
            grad_query
            + jnp.einsum("shqk,skhd->sqhd", mixed, key_rows, preferred_element_type=jnp.float32)
            * score_scale
        )
        key_part = (
            jnp.einsum("shqk,sqhd->skhd", mixed, queries, preferred_element_type=jnp.float32)
            * score_scale
        )
        value_part = jnp.einsum(
            "shqk,sqhd->skhd", probs_bf, grad_context, preferred_element_type=jnp.float32
        )
        start = step * key_block
        grad_keys = lax.dynamic_update_slice_in_dim(
            grad_keys, key_part.reshape(seq_local, key_block, model_width), start, 1
        )
        grad_values = lax.dynamic_update_slice_in_dim(
            grad_values, value_part.reshape(seq_local, key_block, model_width), start, 1
        )
        return (grad_query, grad_keys, grad_values)

    whole_shape = (seq_local, full_len, model_width)
    grad_query, grad_keys, grad_values = lax.fori_loop(
        0,
        key_steps,
        partial_step,
        (
            jnp.zeros(head_shape, jnp.float32),
            jnp.zeros(whole_shape, jnp.float32),
            jnp.zeros(whole_shape, jnp.float32),
        ),
    )
    grad_keys, grad_values = (
        lax.psum_scatter(grad_keys, "seq", scatter_dimension=1, tiled=True),
        lax.psum_scatter(grad_values, "seq", scatter_dimension=1, tiled=True),
    )
    grad_query = grad_query.reshape(row_count, model_width)
    grad_keys = grad_keys.reshape(row_count, model_width)
    grad_values = grad_values.reshape(row_count, model_width)
    grad_qkv_bf = jnp.concatenate(
        [
            grad_query.astype(jnp.bfloat16),
            grad_keys.astype(jnp.bfloat16),
            grad_values.astype(jnp.bfloat16),
        ],
        axis=1,
    )
    grad_qkv = jnp.einsum("nd,nc->dc", flat_in, grad_qkv_bf, preferred_element_type=jnp.float32)
    input_grad = (
        grad_first
        + jnp.einsum("nc,dc->nd", grad_qkv_bf, qkv_back, preferred_element_type=jnp.float32)
    ).reshape(flat_shape)
    shares = (
        lax.psum_scatter(grad_qkv * grad_scale, "fsdp", scatter_dimension=0, tiled=True),
        lax.psum_scatter(
            jnp.sum(grad_query, axis=0) * grad_scale, "fsdp", scatter_dimension=0, tiled=True
        ),
        lax.psum_scatter(
            jnp.sum(grad_values, axis=0) * grad_scale, "fsdp", scatter_dimension=0, tiled=True
        ),
        lax.psum_scatter(grad_out * grad_scale, "fsdp", scatter_dimension=0, tiled=True),
        lax.psum_scatter(
            jnp.sum(grad_first, axis=0) * grad_scale, "fsdp", scatter_dimension=0, tiled=True
        ),
        lax.psum_scatter(grad_gain_one * grad_scale, "fsdp", scatter_dimension=0, tiled=True),
        lax.psum_scatter(grad_shift_one * grad_scale, "fsdp", scatter_dimension=0, tiled=True),
        lax.psum_scatter(grad_up * grad_scale, "fsdp", scatter_dimension=0, tiled=True),
        lax.psum_scatter(
            jnp.sum(grad_pre, axis=0) * grad_scale, "fsdp", scatter_dimension=0, tiled=True
        ),
        lax.psum_scatter(grad_down * grad_scale, "fsdp", scatter_dimension=0, tiled=True),
        lax.psum_scatter(
            jnp.sum(grad_second, axis=0) * grad_scale, "fsdp", scatter_dimension=0, tiled=True
        ),
        lax.psum_scatter(grad_gain_two * grad_scale, "fsdp", scatter_dimension=0, tiled=True),
        lax.psum_scatter(grad_shift_two * grad_scale, "fsdp", scatter_dimension=0, tiled=True),
    )
    (
        share_qkv,
        share_bq,
        share_bv,
        share_out,
        share_bout,
        share_gone,
        share_sone,
        share_up,
        share_bup,
        share_down,
        share_bdown,
        share_gtwo,
        share_stwo,
    ) = shares
    totals = lax.psum(
        (
            share_qkv,
            share_bq,
            share_bv,
            share_out,
            share_bout,
            share_gone,
            share_sone,
            share_up,
            share_bup,
            share_down,
            share_bdown,
            share_gtwo,
            share_stwo,
        ),
        "seq",
    )
    return (encoded, input_grad) + tuple(totals)


def solution(mesh):
    placed = (
        P("fsdp", "seq", None),
        P("fsdp"),
        P(),
        P("fsdp", None),
        P("fsdp"),
        P("fsdp"),
        P("fsdp", None),
        P("fsdp"),
        P("fsdp"),
        P("fsdp"),
        P("fsdp", None),
        P("fsdp"),
        P("fsdp", None),
        P("fsdp"),
        P("fsdp"),
        P("fsdp"),
        P("fsdp", "seq", None),
    )
    return jax.shard_map(
        body,
        mesh=mesh,
        in_specs=placed,
        out_specs=(
            P("fsdp", "seq", None),
            P("fsdp", "seq", None),
            P("fsdp", None),
            P("fsdp"),
            P("fsdp"),
            P("fsdp", None),
            P("fsdp"),
            P("fsdp"),
            P("fsdp"),
            P("fsdp", None),
            P("fsdp"),
            P("fsdp", None),
            P("fsdp"),
            P("fsdp"),
            P("fsdp"),
        ),
        check_vma=False,
    )
```

profile of v0, /device:TPU:0, one launch (start us, length us, event | category | flops | bytes accessed | tf_op | source)
XLA Modules:
  0.0 975.9 jit_solution(3698081270685210517)
XLA Ops:
  8.0 1.3 fusion.71
  16.6 13.9 %all-reduce.20 = (bf16[768]{0:T(1024)(128)(2,1)S(1)}, bf16[768]{0:T(1024)(128)(2,1)S(1)}, bf16[768]{0:T(1024)(128)(2,1)S(1)}, bf16[768]{0:T(1024)(128)(2,1)S(1)}...) all-reduce(bf16[768]{0:T(1024)(128)(2,1)S(1)} %dynamic-update-slice, ...), channel_id=1, replica_groups=mesh['seq'=8,'fsdp'=4] {'fsdp'}, use_global_device_ids=true, to_apply=%add | all-reduce | flops 6144 | bytes 24576
  30.5 12.7 %all-gather.10.cloned.1.call-done = bf16[768,2304]{1,0:T(8,128)(2,1)} async-done(((bf16[192,2304]{1,0:T(8,128)(2,1)}), bf16[768,2304]{1,0:T(8,128)(2,1)}) %all-gather.10.cloned.1.call-update) | async-done | bytes 3538960 | tf_op jit(solution)/shard_map/all_gather | solution.py:76
  43.3 2.8 fusion.55
  50.0 5.4 all-gather.2
  58.1 33.1 %all-gather.18.cloned.1.call-done = bf16[1024,768]{1,0:T(8,128)(2,1)} async-done(((bf16[128,768]{1,0:T(8,128)(2,1)}), bf16[1024,768]{1,0:T(8,128)(2,1)}) %all-gather.18.cloned.1.call-update) | async-done | bytes 1572880 | tf_op jit(solution)/shard_map/all_gather | solution.py:101
  91.2 2.6 copy.52
  93.8 42.8 %all-gather.20.cloned.1.call-done = bf16[1024,768]{1,0:T(8,128)(2,1)} async-done(((bf16[128,768]{1,0:T(8,128)(2,1)}), bf16[1024,768]{1,0:T(8,128)(2,1)}) %all-gather.20.cloned.1.call-update) | async-done | bytes 1572880 | tf_op jit(solution)/shard_map/all_gather | solution.py:100
  136.5 2.6 copy.53
  139.1 6.0 while.48
  145.2 7.7 while.49
  145.2 1.5 constant_dynamic-slice_fusion.10
  146.8 1.5 fusion.119
  149.1 1.5 constant_dynamic-slice_fusion.10
  150.6 1.5 fusion.119
  154.0 1.7 fusion.72
  155.9 36.7 %all-gather.14.cloned.1.call-done = bf16[768,3072]{1,0:T(8,128)(2,1)} async-done(((bf16[192,3072]{1,0:T(8,128)(2,1)}), bf16[768,3072]{1,0:T(8,128)(2,1)}) %all-gather.14.cloned.1.call-update) | async-done | bytes 4718608 | tf_op jit(solution)/shard_map/all_gather | solution.py:78
  192.7 3.2 convolution_add_fusion
  195.9 35.6 %all-gather.16.cloned.1.call-done = bf16[3072,768]{1,0:T(8,128)(2,1)} async-done(((bf16[768,768]{1,0:T(8,128)(2,1)}), bf16[3072,768]{1,0:T(8,128)(2,1)}) %all-gather.16.cloned.1.call-update) | async-done | bytes 4718608 | tf_op jit(solution)/shard_map/all_gather | solution.py:79
  231.5 3.5 fusion.73
  236.0 1.5 fusion.66
  237.5 2.3 fusion.74
  239.8 2.3 multiply_reduce_fusion
  244.5 2.0 broadcast.243
  246.6 2.1 broadcast.243.clone
  248.6 31.8 %while.50 = (s32[]{:T(128)}, f32[1,128,12,64]{1,3,2,0:T(8,128)S(1)}, f32[1,1024,768]{1,2,0:T(8,128)}, f32[1,1024,768]{1,2,0:T(8,128)}, bf16[1,1024,768]{1,2,0:T(...) while((s32[]{:T(128)}, ...), condition=%wide.region_15.16_spmd.clone, body=%wide.region_14.15_spmd.clone.sunk | while | flops 513441792 | bytes 107860536 | solution.py:247
  251.2 1.8 constant_dynamic-slice_fusion.12
  253.0 2.4 multiply_convert_fusion.5
  255.9 1.4 copy-done.1
  257.3 2.2 fusion.132
  261.9 1.6 copy-done.7
  267.1 1.8 constant_dynamic-slice_fusion.12
  268.9 2.4 multiply_convert_fusion.5
  271.8 1.4 copy-done.1
  273.2 2.2 fusion.132
  277.8 1.6 copy-done.7
  282.0 73.4 %reduce-scatter.11.cloned.1.call-done = f32[1,128,768]{1,2,0:T(8,128)} async-done(((f32[1,1024,768]{1,2,0:T(8,128)}), f32[1,128,768]{1,2,0:T(8,128)}) %reduce-scatter.11.cloned.1.call-update) | async-done | bytes 393232 | tf_op jit(solution)/shard_map/reduce_scatter | solution.py:259
  355.5 1.9 fusion.69
  357.3 75.7 %reduce-scatter.9.cloned.1.call-done = f32[1,128,768]{1,2,0:T(8,128)} async-done(((f32[1,1024,768]{1,2,0:T(8,128)}), f32[1,128,768]{1,2,0:T(8,128)}) %reduce-scatter.9.cloned.1.call-update) | async-done | bytes 393232 | tf_op jit(solution)/shard_map/reduce_scatter | solution.py:258
  434.1 4.0 multiply_bitcast_fusion
  438.1 8.1 copy.67
  447.2 1.9 convolution_multiply_fusion.5
  449.1 5.9 convolution_multiply_fusion.3
  455.1 2.0 copy-done.3
  457.3 5.1 convolution_multiply_fusion.2
  462.5 47.1 %reduce-scatter.19.cloned.1.call-done = f32[192,2304]{1,0:T(8,128)} async-done(((f32[768,2304]{1,0:T(8,128)}), f32[192,2304]{1,0:T(8,128)}) %reduce-scatter.19.cloned.1.call-update) | async-done | bytes 1769488
  509.6 2.9 copy.68
  512.6 32.9 %reduce-scatter.13.cloned.1.call-done = f32[192,768]{1,0:T(8,128)} async-done(((f32[768,768]{1,0:T(8,128)}), f32[192,768]{1,0:T(8,128)}) %reduce-scatter.13.cloned.1.call-update) | async-done | bytes 589840 | tf_op jit(solution)/shard_map/reduce_scatter | solution.py:285
  545.4 80.5 %reduce-scatter.15.cloned.1.call-done = f32[192,3072]{1,0:T(8,128)} async-done(((f32[768,3072]{1,0:T(8,128)}), f32[192,3072]{1,0:T(8,128)}) %reduce-scatter.15.cloned.1.call-update) | async-done | bytes 2359312 | tf_op jit(solution)/shard_map/reduce_scatter | solution.py:291
  626.0 80.4 %reduce-scatter.17.cloned.1.call-done = f32[768,768]{1,0:T(8,128)} async-done(((f32[3072,768]{1,0:T(8,128)}), f32[768,768]{1,0:T(8,128)}) %reduce-scatter.17.cloned.1.call-update) | async-done | bytes 2359312 | tf_op jit(solution)/shard_map/reduce_scatter | solution.py:295
  714.8 1.3 broadcast_multiply_fusion.3
  716.8 1.3 broadcast_multiply_fusion.8
  718.0 12.4 %all-reduce.19 = (f32[768]{0:T(1024)}, f32[768]{0:T(1024)}, f32[768]{0:T(1024)}, f32[768]{0:T(1024)}, f32[768]{0:T(1024)}, /*index=5*/f32[3072]{0:T(1024)}, f32[768]{0:T(1024)}, f32[768]{0:T(1024)}, f32[768]{0:T(1024)}) all-reduce(f32[768]{0:T(1024)} %mul.317, ...), channel_id=7, replica_groups=mesh['seq'=8,'fsdp'=4] {'fsdp'}, use_global_device_ids=true, to_apply=%region_21.22.clone | all-reduce | flops 9216 | bytes 73728
  732.7 1.3 dynamic-slice.15
  734.0 1.3 dynamic-slice.17
  735.3 1.3 dynamic-slice.21
  736.7 1.3 dynamic-slice.23
  738.0 1.3 dynamic-slice.25
  740.1 39.5 %all-reduce.17 = (f32[192]{0:T(256)}, f32[192]{0:T(256)}, f32[192]{0:T(256)}, f32[192]{0:T(256)}, f32[192]{0:T(256)}, /*index=5*/f32[768]{0:T(1024)}, f32[192]{0:T(256)}, f32[192]{0:T(256)}, f32[192]{0:T(256)}) all-reduce(f32[192]{0:T(256)S(1)} %dynamic-slice.9, ...), channel_id=1, replica_groups=mesh['seq'=8,'fsdp'=4] {'seq'}, use_global_device_ids=true, to_apply=%region_22.23 | all-reduce | flops 2304 | bytes 18432 | tf_op jit(solution)/shard_map/psum | solution.py:317
  779.5 3.3 fusion.36
  782.9 178.7 %all-reduce.23.cloned.1.call-done = (f32[192,2304]{0,1:T(8,128)}, f32[192,768]{1,0:T(8,128)}, f32[192,3072]{1,0:T(8,128)}, f32[768,768]{1,0:T(8,128)}) async-done(((f32[192,2304]{0,1:T(8,128)}, f32[192,768]{1,0:T(8,128)}, f32[192,3072]{1,0:T(8,128)}, f32[768,768]{1,0:T(8,128)}), (f32[192,2304]{0,1:T(8,128)}, f32[192,768]{1,0:T(8,128)}, f32[192,3072]{1,0:T(8,128)}, ...) | async-done | bytes 7077904 | tf_op jit(solution)/shard_map/psum | solution.py:317
  961.6 3.1 copy.58
  965.5 1.4 copy.116
  968.0 1.4 copy.117
  (247 shorter events, 54.7 us)
Async XLA Ops:
  7.2 36.1 %all-gather.10.cloned.1.call-start = ((), (), s32[]{:S(2)}) async-start(), calls=%async_computation.6 | async-start | bytes 4423680 | tf_op jit(solution)/shard_map/all_gather | solution.py:76
  7.9 83.3 %all-gather.18.cloned.1.call-start = ((), (), s32[]{:S(2)}) async-start(), calls=%async_computation.15 | async-start | bytes 1769472 | tf_op jit(solution)/shard_map/all_gather | solution.py:101
  46.0 4.0 copy-start.46
  46.0 11.2 %copy-start.47 = (s32[8]{0:T(128)S(1)}, s32[8]{0:T(128)}, u32[]{:S(2)}) copy-start(s32[8]{0:T(128)} %param.25) | copy-start | bytes 100
  46.8 89.7 %all-gather.20.cloned.1.call-start = ((), (), s32[]{:S(2)}) async-start(), calls=%async_computation.16 | async-start | bytes 1769472 | tf_op jit(solution)/shard_map/all_gather | solution.py:100
  47.6 106.3 %all-gather.12.cloned.1.call-start = ((), (), s32[]{:S(2)}) async-start(), calls=%async_computation.7 | async-start | bytes 1474560 | tf_op jit(solution)/shard_map/all_gather | solution.py:77
  48.2 144.5 %all-gather.14.cloned.1.call-start = ((), (), s32[]{:S(2)}) async-start(), calls=%async_computation.8 | async-start | bytes 5898240 | tf_op jit(solution)/shard_map/all_gather | solution.py:78
  48.8 182.8 %all-gather.16.cloned.1.call-start = ((), (), s32[]{:S(2)}) async-start(), calls=%async_computation.9 | async-start | bytes 5898240 | tf_op jit(solution)/shard_map/all_gather | solution.py:79
  49.3 306.1 %reduce-scatter.11.cloned.1.call-start = ((), (), s32[]{:S(2)}) async-start(), calls=%async_computation.11 | async-start | bytes 3538944 | tf_op jit(solution)/shard_map/reduce_scatter | solution.py:259
  145.2 8.8 copy-start.20
  145.2 8.8 copy-start.41
  152.9 39.8 %copy-start.33 = (f32[4,1,768]{2,1,0:T(1,128)S(1)}, f32[4,1,768]{2,1,0:T(1,128)}, u32[]{:S(2)}) copy-start(f32[4,1,768]{2,1,0:T(1,128)} %convert_element_type.142) | copy-start | bytes 36868
  153.9 38.7 %copy-start.22 = (bf16[1,128,12,64]{1,3,2,0:T(8,128)(2,1)}, bf16[1,128,12,64]{1,3,2,0:T(8,128)(2,1)S(1)}, u32[]{:S(2)}) copy-start(bf16[1,128,12,64]{1,3,2,0:T(8,128)(2,1)S(1)} %convert_element_type.116) | copy-start | bytes 589828
  155.7 86.5 %copy-start.35 = (f32[128]{0:T(128)}, f32[128]{0:T(128)S(1)}, u32[]{:S(2)}) copy-start(f32[128]{0:T(128)S(1)} %broadcast_multiply_fusion.14) | copy-start | bytes 1540
  155.9 86.3 %copy-start.37 = (f32[128]{0:T(128)}, f32[128]{0:T(128)S(1)}, u32[]{:S(2)}) copy-start(f32[128]{0:T(128)S(1)} %add_rsqrt_fusion.1) | copy-start | bytes 1540
  192.7 38.9 %copy-start.39 = (f32[768]{0:T(1024)S(1)}, f32[768]{0:T(1024)}, u32[]{:S(2)}) copy-start(f32[768]{0:T(1024)} %convert_element_type.123) | copy-start | bytes 9220
  195.9 41.6 %copy-start.2 = (f32[128,3072]{1,0:T(8,128)}, f32[128,3072]{1,0:T(8,128)S(1)}, u32[]{:S(2)}) copy-start(f32[128,3072]{1,0:T(8,128)S(1)} %convolution_add_fusion) | copy-start | bytes 4718596
  195.9 39.4 %copy-start.21 = (bf16[1,128,768]{2,1,0:T(8,128)(2,1)S(1)}, bf16[1,128,768]{2,1,0:T(8,128)(2,1)}, u32[]{:S(2)}) copy-start(bf16[1,128,768]{2,1,0:T(8,128)(2,1)} %param.39) | copy-start | bytes 589828
  195.9 40.1 %copy-start.40 = (f32[768]{0:T(1024)S(1)}, f32[768]{0:T(1024)}, u32[]{:S(2)}) copy-start(f32[768]{0:T(1024)} %convert_element_type.125) | copy-start | bytes 9220
  231.5 6.0 copy-start.12
  236.0 3.8 slice-start
  237.5 2.3 copy-start.14
  237.5 2.3 slice-start.1
  239.8 2.4 copy-start.16
  239.8 3.9 copy-start.13
  242.2 2.2 copy-start.29
  246.6 2.1 copy-start.5
  248.6 2.5 copy-start.42
  248.6 2.5 copy-start.44
  251.2 4.2 copy-start
  257.3 2.9 copy-start.8
  259.5 1.9 copy-start.6
  261.4 3.1 copy-start.31
  261.4 3.1 copy-start.43
  261.4 3.2 copy-start.45
  261.9 2.6 copy-start.9
  264.5 2.5 copy-start.42
  264.5 2.5 copy-start.44
  267.1 4.2 copy-start
  273.2 2.9 copy-start.8
  275.4 1.9 copy-start.6
  277.3 3.2 copy-start.31
  277.3 3.2 copy-start.43
  277.3 3.2 copy-start.45
  277.8 2.6 copy-start.9
  280.4 152.6 %reduce-scatter.9.cloned.1.call-start = ((), (), s32[]{:S(2)}) async-start(), calls=%async_computation.10 | async-start | bytes 3538944 | tf_op jit(solution)/shard_map/reduce_scatter | solution.py:258
  281.2 228.4 %reduce-scatter.19.cloned.1.call-start = ((), (), s32[]{:S(2)}) async-start(), calls=%async_computation.17 | async-start | bytes 8847360
  282.0 156.0 %copy-start.24 = (bf16[1,128,12,64]{1,3,2,0:T(8,128)(2,1)}, bf16[1,128,12,64]{1,3,2,0:T(8,128)(2,1)S(1)}, u32[]{:S(2)}) copy-start(bf16[1,128,12,64]{1,3,2,0:T(8,128)(2,1)S(1)} %get-tuple-element.740) | copy-start | bytes 589828
  357.3 80.7 %copy-start.25 = (bf16[128,768]{0,1:T(8,128)(2,1)}, bf16[128,768]{0,1:T(8,128)(2,1)S(1)}, u32[]{:S(2)}) copy-start(bf16[128,768]{0,1:T(8,128)(2,1)S(1)} %get-tuple-element.738) | copy-start | bytes 589828
  434.1 4.0 copy-start.26
  446.2 3.0 copy-start.17
  446.2 3.0 copy-start.36
  446.2 2.9 copy-start.38
  446.2 99.2 %reduce-scatter.13.cloned.1.call-start = ((), (), s32[]{:S(2)}) async-start(), calls=%async_computation.12 | async-start | bytes 2949120 | tf_op jit(solution)/shard_map/reduce_scatter | solution.py:285
  449.1 176.9 %reduce-scatter.15.cloned.1.call-start = ((), (), s32[]{:S(2)}) async-start(), calls=%async_computation.13 | async-start | bytes 11796480 | tf_op jit(solution)/shard_map/reduce_scatter | solution.py:291
  455.0 2.1 copy-start.3
  455.0 2.3 copy-start.15
  455.0 251.4 %reduce-scatter.17.cloned.1.call-start = ((), (), s32[]{:S(2)}) async-start(), calls=%async_computation.14 | async-start | bytes 11796480 | tf_op jit(solution)/shard_map/reduce_scatter | solution.py:295
  462.4 499.2 %all-reduce.23.cloned.1.call-start = ((), (), s32[]{:S(2)}) async-start(), calls=%async_computation.18 | async-start | bytes 15335424 | tf_op jit(solution)/shard_map/psum | solution.py:317
  706.4 3.2 copy-start.34
  706.4 73.2 %copy-start.4 = (bf16[768,2304]{1,0:T(8,128)(2,1)S(1)}, bf16[768,2304]{1,0:T(8,128)(2,1)}, u32[]{:S(2)}) copy-start(bf16[768,2304]{1,0:T(8,128)(2,1)} %all-gather.10.cloned.1.call-done) | copy-start | bytes 10616836
  961.6 3.1 copy-start.32
  961.6 3.9 copy-start.19
  965.5 2.5 copy-start.18
  (13 other events, 15.9 us)
Sparse Core Ops, SparseCore 0:
  9.5 33.6 all-gather.9
  46.9 44.2 all-gather.17
  94.0 42.5 all-gather.19
  137.9 15.7 all-gather.11
  155.2 37.4 all-gather.13
  194.1 37.4 all-gather.15
  280.6 74.8 reduce-scatter.10
  359.1 73.9 reduce-scatter.8
  446.3 63.2 reduce-scatter.18
  512.6 32.8 reduce-scatter.12
  548.0 77.8 reduce-scatter.14
  628.4 77.9 reduce-scatter.16
  711.5 250.0 all-reduce.22
where the time goes:
time: 978 us; the launch traced here: 976 us
  waiting for transfers between devices  733 us (75%)
  local copies, waits for them, and re-layouts  77.2 us (8%)
  blocking collectives  71.1 us (7%)
  matrix products  53.9 us (6%)
  other arithmetic  22.5 us (2%)
  between operations  17.3 us (2%)
    psum x1, waiting for transfers between devices, body(): lax.psum((share_qkv, share_bq, share_bv, share_out, share_bout, share_gon...  179 us
    reduce_scatter x1, waiting for transfers between devices, body(): lax.psum_scatter(grad_up * grad_scale, 'fsdp', scatter_dimension=0, tiled...  80.5 us
    reduce_scatter x1, waiting for transfers between devices, body(): lax.psum_scatter(grad_down * grad_scale, 'fsdp', scatter_dimension=0, til...  80.4 us
    reduce_scatter x1, waiting for transfers between devices, body(): lax.psum_scatter(grad_keys, 'seq', scatter_dimension=1, tiled=True)  75.7 us
    reduce_scatter x1, waiting for transfers between devices, body(): lax.psum_scatter(grad_values, 'seq', scatter_dimension=1, tiled=True)  73.4 us
    unnamed x14, waiting for transfers between devices  50.2 us
    unnamed x108, local copies, waits for them, and re-layouts  45.6 us
    all_gather x1, waiting for transfers between devices, body(): lax.all_gather(keys_own, 'seq', axis=1, tiled=True)  42.8 us
  transfers between devices with their start and end apart: 13, of which 12 were waited for; matrix products, arithmetic and copies ran while one was open for 8% of the time, Pallas kernels for 0%

commit v1 on v0

v1 whole, which is shorter than its diff:
```python
import functools

import jax
import jax.numpy as jnp
from jax import lax
from jax.experimental import pallas as pl
from jax.experimental.pallas import tpu as pltpu
from jax.sharding import PartitionSpec as P

HEADS = 12

epsilon = 1e-06
masked_out = -1e30
bf16 = jnp.bfloat16
f32 = jnp.float32


def norm_forward(hidden, gain, shift):
    centre = hidden - jnp.mean(hidden, axis=-1, keepdims=True)
    spread = lax.rsqrt(jnp.mean(centre * centre, axis=-1, keepdims=True) + epsilon)
    normed = centre * spread
    return (normed * gain + shift, normed, spread)


def norm_backward(upstream, normed, spread, gain):
    scaled = upstream * gain
    grad_in = spread * (
        scaled
        - jnp.mean(scaled, axis=-1, keepdims=True)
        - normed * jnp.mean(scaled * normed, axis=-1, keepdims=True)
    )
    return (grad_in, jnp.sum(upstream * normed, axis=0), jnp.sum(upstream, axis=0))


def gelu_exact(pre):
    return 0.5 * pre * (1.0 + lax.erf(pre * 0.7071067811865476))


def gelu_slope(pre):
    return (
        0.5 * (1.0 + lax.erf(pre * 0.7071067811865476))
        + pre * jnp.exp(-0.5 * pre * pre) * 0.3989422804014327
    )


def swap(value, axis, mask):
    count = lax.axis_size(axis)
    return lax.ppermute(value, axis, [(i, i ^ mask) for i in range(count)])


def masks_of(count):
    found = []
    bit = count // 2
    while bit:
        found.append(bit)
        bit //= 2
    return found


def relative_order(count):
    order = [0]
    for mask in masks_of(count):
        order = order + [item ^ mask for item in order]
    return order


def gather_rows(value, axis):
    for mask in masks_of(lax.axis_size(axis)):
        value = jnp.concatenate([value, swap(value, axis, mask)], axis=0)
    return value


def scatter_rows(partial, axis):
    for mask in reversed(masks_of(lax.axis_size(axis))):
        half = partial.shape[0] // 2
        sent = swap(partial[half:].astype(bf16), axis, mask)
        partial = partial[:half].astype(f32) + sent.astype(f32)
    return partial


def pick(stack, index):
    return lax.dynamic_index_in_dim(stack, index, 0, keepdims=False)


def reorder(stack, base):
    return jnp.stack([pick(stack, base ^ g) for g in range(stack.shape[0])])


def exchange(stack, axis, base, stride, count):
    return [pick(stack, base)] + [
        swap(pick(stack, base ^ m), axis, m * stride) for m in range(1, count)
    ]


def attend_kernel(heads, size, scale, q_ref, k_ref, v_ref, bias_ref, ctx_ref, lse_ref):
    bias = bias_ref[...]
    lanes = lax.broadcasted_iota(jnp.int32, lse_ref.shape, 1)
    stats = jnp.zeros(lse_ref.shape, f32)
    outs = []
    for h in range(heads):
        cols = slice(h * size, (h + 1) * size)
        logits = (
            lax.dot_general(
                q_ref[:, cols], k_ref[:, cols], (((1,), (1,)), ((), ())), preferred_element_type=f32
            )
            * scale
            + bias
        )
        top = jnp.max(logits, axis=-1, keepdims=True)
        terms = jnp.exp(logits - top)
        total = jnp.sum(terms, axis=-1, keepdims=True)
        context = jnp.dot(terms.astype(bf16), v_ref[:, cols], preferred_element_type=f32)
        outs.append(context / total)
        stats = jnp.where(lanes == h, top + jnp.log(total), stats)
    ctx_ref[...] = jnp.concatenate(outs, axis=1).astype(bf16)
    lse_ref[...] = stats


def attend(queries, keys, values, bias, heads):
    rows, width = queries.shape
    full_len = keys.shape[0]
    size = width // heads
    tile = min(128, rows)
    whole = lambda i: (0, 0)
    return pl.pallas_call(
        functools.partial(attend_kernel, heads, size, size ** (-0.5)),
        grid=(rows // tile,),
        in_specs=[
            pl.BlockSpec((tile, width), lambda i: (i, 0)),
            pl.BlockSpec((full_len, width), whole),
            pl.BlockSpec((full_len, width), whole),
            pl.BlockSpec((1, full_len), whole),
        ],
        out_specs=[
            pl.BlockSpec((tile, width), lambda i: (i, 0)),
            pl.BlockSpec((tile, 128), lambda i: (i, 0)),
        ],
        out_shape=[
            jax.ShapeDtypeStruct((rows, width), bf16),
            jax.ShapeDtypeStruct((rows, 128), f32),
        ],
        cost_estimate=pl.CostEstimate(
            flops=4 * rows * full_len * width,
            bytes_accessed=4 * (rows + full_len) * width,
            transcendentals=rows * full_len * heads,
        ),
        name="attend",
    )(queries, keys, values, bias)


def attend_back_kernel(
    heads, size, scale, q_ref, k_ref, v_ref, bias_ref, lse_ref, ctx_ref, g_ref, dq_ref, dk_ref, dv_ref
):
    @pl.when(pl.program_id(0) == 0)
    def _():
        dk_ref[...] = jnp.zeros_like(dk_ref)
        dv_ref[...] = jnp.zeros_like(dv_ref)

    bias = bias_ref[...]
    dqs, dks, dvs = [], [], []
    for h in range(heads):
        cols = slice(h * size, (h + 1) * size)
        q_h, k_h, v_h, g_h = q_ref[:, cols], k_ref[:, cols], v_ref[:, cols], g_ref[:, cols]
        logits = (
            lax.dot_general(q_h, k_h, (((1,), (1,)), ((), ())), preferred_element_type=f32) * scale
            + bias
        )
        probs = jnp.exp(logits - lse_ref[:, h : h + 1])
        grad_logit = lax.dot_general(
            g_h, v_h, (((1,), (1,)), ((), ())), preferred_element_type=f32
        )
        correction = jnp.sum(
            g_h.astype(f32) * ctx_ref[:, cols].astype(f32), axis=-1, keepdims=True
        )
        mixed = (probs * (grad_logit - correction)).astype(bf16)
        dqs.append(jnp.dot(mixed, k_h, preferred_element_type=f32) * scale)
        dks.append(
            lax.dot_general(mixed, q_h, (((0,), (0,)), ((), ())), preferred_element_type=f32)
            * scale
        )
        dvs.append(
            lax.dot_general(
                probs.astype(bf16), g_h, (((0,), (0,)), ((), ())), preferred_element_type=f32
            )
        )
    dq_ref[...] = jnp.concatenate(dqs, axis=1)
    dk_ref[...] += jnp.concatenate(dks, axis=1)
    dv_ref[...] += jnp.concatenate(dvs, axis=1)


def attend_back(queries, keys, values, bias, lse, context, grad, heads):
    rows, width = queries.shape
    full_len = keys.shape[0]
    size = width // heads
    tile = min(128, rows)
    whole = lambda i: (0, 0)
    part = lambda i: (i, 0)
    return pl.pallas_call(
        functools.partial(attend_back_kernel, heads, size, size ** (-0.5)),
        grid=(rows // tile,),
        in_specs=[
            pl.BlockSpec((tile, width), part),
            pl.BlockSpec((full_len, width), whole),
            pl.BlockSpec((full_len, width), whole),
            pl.BlockSpec((1, full_len), whole),
            pl.BlockSpec((tile, 128), part),
            pl.BlockSpec((tile, width), part),
            pl.BlockSpec((tile, width), part),
        ],
        out_specs=[
            pl.BlockSpec((tile, width), part),
            pl.BlockSpec((full_len, width), whole),
            pl.BlockSpec((full_len, width), whole),
        ],
        out_shape=[
            jax.ShapeDtypeStruct((rows, width), f32),
            jax.ShapeDtypeStruct((full_len, width), f32),
            jax.ShapeDtypeStruct((full_len, width), f32),
        ],
        cost_estimate=pl.CostEstimate(
            flops=10 * rows * full_len * width,
            bytes_accessed=8 * (rows + full_len) * width,
            transcendentals=rows * full_len * heads,
        ),
        name="attend_back",
    )(queries, keys, values, bias, lse, context, grad)


def dot(a, b):
    return jnp.dot(a, b, preferred_element_type=f32)


def dot_nt(a, b):
    return lax.dot_general(a, b, (((1,), (1,)), ((), ())), preferred_element_type=f32)


def dot_tn(a, b):
    return lax.dot_general(a, b, (((0,), (0,)), ((), ())), preferred_element_type=f32)


def halve_sum(chunks, axis):
    me = lax.axis_index(axis)
    for level, mask in enumerate(reversed(masks_of(lax.axis_size(axis)))):
        bit = (me >> level) & 1
        paired = chunks.reshape((chunks.shape[0] // 2, 2) + chunks.shape[1:])
        kept = lax.dynamic_index_in_dim(paired, bit, 1, keepdims=False)
        sent = lax.dynamic_index_in_dim(paired, 1 - bit, 1, keepdims=False)
        chunks = (kept.astype(f32) + swap(sent, axis, mask).astype(f32)).astype(bf16)
    return chunks[0]


def double_gather(chunk, axis):
    me = lax.axis_index(axis)
    masks = masks_of(lax.axis_size(axis))
    chunks = chunk[None, None]
    for level, mask in zip(reversed(range(len(masks))), masks):
        bit = (me >> level) & 1
        other = swap(chunks, axis, mask)
        low = jnp.where(bit == 0, chunks, other)
        high = jnp.where(bit == 0, other, chunks)
        chunks = jnp.concatenate([low, high], axis=1)
        chunks = chunks.reshape((chunks.shape[0] * 1,) + chunks.shape[1:])
        chunks = chunks.reshape((chunks.shape[0] * chunks.shape[1], 1) + chunks.shape[2:])
    return chunks[:, 0]


def sum_small(value, axes):
    for axis in axes:
        for mask in masks_of(lax.axis_size(axis)):
            value = value + swap(value, axis, mask)
    return value


def body(
    tokens,
    lengths,
    block_order,
    qkv_weight,
    q_bias,
    v_bias,
    out_weight,
    out_bias,
    norm1_gain,
    norm1_shift,
    up_weight,
    up_bias,
    down_weight,
    down_bias,
    norm2_gain,
    norm2_shift,
    cotangent,
):
    seq_local, block_len, model_width = tokens.shape
    seq_count = lax.axis_size("seq")
    fsdp_count = lax.axis_size("fsdp")
    me_f = lax.axis_index("fsdp")
    me_s = lax.axis_index("seq")
    stride = seq_count // fsdp_count
    zone = me_s // stride
    lane = me_s % stride
    part_width = model_width // fsdp_count
    heads_own = HEADS // fsdp_count
    grad_scale = (block_len * seq_local * seq_count * fsdp_count) ** (-0.5)
    order = relative_order(fsdp_count)

    def columns(weight, pieces):
        rows, total = weight.shape
        split = weight.reshape(rows, pieces, fsdp_count, total // (pieces * fsdp_count))
        split = jnp.moveaxis(split, 2, 0).reshape(fsdp_count, rows, total // fsdp_count)
        return exchange(split, "fsdp", me_f, 1, fsdp_count)

    flat_in = tokens.reshape(block_len, model_width)
    all_in = gather_rows(flat_in, "fsdp")
    qkv_own = reorder(jnp.stack(columns(qkv_weight, 3)), me_f).reshape(model_width, 3 * part_width)

    vectors = jnp.stack(
        [item.astype(f32) for item in (out_bias, norm1_gain, norm1_shift, down_bias, norm2_gain, norm2_shift)]
        + [jnp.broadcast_to(lengths.astype(f32), (part_width,))]
    )
    vectors = gather_rows(vectors[None], "fsdp")
    length = pick(vectors, zone)[-1, 0].astype(jnp.int32)
    inverse = [order.index(r) for r in range(fsdp_count)]
    by_relative = jnp.stack([vectors[inverse[r]] for r in range(fsdp_count)])
    full = jnp.moveaxis(reorder(by_relative, me_f), 0, 1).reshape(-1, model_width)
    bias_out, gain_one, shift_one, bias_down, gain_two, shift_two = [full[i] for i in range(6)]

    projected = dot(all_in, qkv_own)
    added = jnp.concatenate(
        [q_bias.astype(f32), jnp.zeros((part_width,), f32), v_bias.astype(f32)]
    )
    qkv = (projected + added).astype(bf16).reshape(fsdp_count, block_len, 3 * part_width)
    arrived = exchange(qkv, "seq", zone, stride, fsdp_count)
    queries = jnp.concatenate([item[:, :part_width] for item in arrived], axis=0)
    pairs = [item[:, part_width:] for item in arrived]
    pairs = jnp.concatenate(
        [item if r == 0 else swap(item, "seq", r) for r in range(stride) for item in pairs], axis=0
    )
    keys, values = pairs[:, :part_width], pairs[:, part_width:]
    source = jnp.stack(
        [((zone ^ m) * stride + (lane ^ r)) for r in range(stride) for m in range(fsdp_count)]
    )
    block_at = jnp.sum(
        jnp.where(
            source[:, None] == jnp.arange(seq_count, dtype=jnp.int32)[None, :], block_order[None, :], 0
        ),
        axis=1,
    )
    position = (
        block_at[:, None] * block_len + jnp.arange(block_len, dtype=jnp.int32)[None, :]
    ).reshape(1, -1)
    bias = jnp.where(position < length, 0.0, masked_out).astype(f32)
    context, lse = attend(queries, keys, values, bias, heads_own)

    up_own = reorder(jnp.stack(columns(up_weight, 1)), me_f).reshape(model_width, -1)

    def home(stack):
        got = [stack[0]] + [swap(stack[m], "seq", m * stride) for m in range(1, fsdp_count)]
        return reorder(jnp.stack(got), zone).reshape(fsdp_count * block_len, -1)

    context_tok = home(context.reshape(fsdp_count, block_len, part_width))
    attended = scatter_rows(dot(context_tok, out_weight), "fsdp") + bias_out
    first_sum = flat_in.astype(f32) + attended
    first_out, first_norm, first_spread = norm_forward(first_sum, gain_one, shift_one)
    first_all = gather_rows(first_out.astype(bf16), "fsdp")
    pre_act = dot(first_all, up_own) + up_bias.astype(f32)
    activated = gelu_exact(pre_act).astype(bf16)
    second_sum = first_out + scatter_rows(dot(activated, down_weight), "fsdp") + bias_down
    second_out, second_norm, second_spread = norm_forward(second_sum, gain_two, shift_two)
    encoded = second_out.astype(bf16).reshape(tokens.shape)
    upstream = cotangent.reshape(block_len, model_width).astype(f32)
    grad_second, grad_gain_two, grad_shift_two = norm_backward(
        upstream, second_norm, second_spread, gain_two
    )
    second_all = gather_rows(grad_second.astype(bf16), "fsdp")
    grad_act = dot_nt(second_all, down_weight)
    grad_pre = grad_act * gelu_slope(pre_act)
    grad_pre_bf = grad_pre.astype(bf16)
    grad_first_out = grad_second + scatter_rows(dot_nt(grad_pre_bf, up_own), "fsdp")
    grad_down = (dot_tn(activated, second_all) * grad_scale).astype(bf16)
    grad_up = (dot_tn(first_all, grad_pre_bf) * grad_scale).astype(bf16)
    grad_first, grad_gain_one, grad_shift_one = norm_backward(
        grad_first_out, first_norm, first_spread, gain_one
    )
    grad_first_all = gather_rows(grad_first.astype(bf16), "fsdp")
    grad_context = dot_nt(grad_first_all, out_weight).astype(bf16)
    grad_out = (dot_tn(context_tok, grad_first_all) * grad_scale).astype(bf16)
    grad_up_rows = jnp.stack(
        exchange(grad_up.reshape(fsdp_count, part_width, -1), "fsdp", me_f, 1, fsdp_count)
    )
    sum_down, sum_up, sum_out = lax.psum((grad_down, grad_up_rows, grad_out), "seq")

    grad_ctx = jnp.concatenate(
        exchange(grad_context.reshape(fsdp_count, block_len, part_width), "seq", zone, stride, fsdp_count),
        axis=0,
    )
    dq, dk, dv = attend_back(queries, keys, values, bias, lse, context, grad_ctx, heads_own)
    rows = fsdp_count * block_len
    dkv = jnp.concatenate([dk, dv], axis=1)
    dkv_own = dkv[:rows]
    for r in range(1, stride):
        dkv_own = dkv_own + swap(dkv[r * rows : (r + 1) * rows].astype(bf16), "seq", r).astype(f32)
    bias_terms = jnp.stack([jnp.sum(dq, axis=0), jnp.sum(dkv_own[:, part_width:], axis=0)])
    dqkv = jnp.concatenate([dq, dkv_own], axis=1).astype(bf16)
    grad_qkv_tok = home(dqkv.reshape(fsdp_count, block_len, 3 * part_width))
    input_grad = grad_first + scatter_rows(dot_nt(grad_qkv_tok, qkv_own), "fsdp")
    grad_qkv = (dot_tn(all_in, grad_qkv_tok) * grad_scale).astype(bf16)

    chunk = part_width // seq_count
    grad_qkv = grad_qkv.reshape(fsdp_count, seq_count, chunk, 3 * part_width)
    piece = halve_sum(jnp.moveaxis(grad_qkv, 1, 0), "seq")
    piece = jnp.stack(exchange(piece, "fsdp", me_f, 1, fsdp_count))
    sum_qkv = double_gather(reorder(piece, me_f), "seq")
    sum_qkv = sum_qkv.reshape(seq_count, fsdp_count, chunk, 3, part_width)
    sum_qkv = sum_qkv.transpose(0, 2, 3, 1, 4).reshape(part_width, 3 * model_width)

    small_all = sum_small(
        jnp.stack(
            [
                jnp.sum(grad_first, axis=0),
                grad_gain_one,
                grad_shift_one,
                jnp.sum(grad_second, axis=0),
                grad_gain_two,
                grad_shift_two,
            ]
        ),
        ("fsdp", "seq"),
    )
    small_own = lax.dynamic_slice_in_dim(small_all, me_f * part_width, part_width, 1) * grad_scale
    bias_sum = sum_small(bias_terms, ("seq",)) * grad_scale
    up_bias_sum = sum_small(jnp.sum(grad_pre, axis=0), ("seq",)) * grad_scale
    up_rows = jnp.moveaxis(reorder(sum_up, me_f), 0, 1).reshape(part_width, -1)

    return (
        encoded,
        input_grad.reshape(tokens.shape),
        sum_qkv.astype(f32),
        bias_sum[0],
        bias_sum[1],
        sum_out.astype(f32),
        small_own[0],
        small_own[1],
        small_own[2],
        up_rows.astype(f32),
        up_bias_sum,
        sum_down.astype(f32),
        small_own[3],
        small_own[4],
        small_own[5],
    )


def solution(mesh):
    rows = P("fsdp", "seq", None)
    matrix = P("fsdp", None)
    vector = P("fsdp")
    return jax.shard_map(
        body,
        mesh=mesh,
        in_specs=(
            rows,
            vector,
            P(),
            matrix,
            vector,
            vector,
            matrix,
            vector,
            vector,
            vector,
            matrix,
            vector,
            matrix,
            vector,
            vector,
            vector,
            rows,
        ),
        out_specs=(
            rows,
            rows,
            matrix,
            vector,
            vector,
            matrix,
            vector,
            vector,
            vector,
            matrix,
            vector,
            matrix,
            vector,
            vector,
            vector,
        ),
        check_vma=False,
    )
```

time: 978 us -> 374 us (0.38)
  waiting for transfers between devices: 733 us -> 196 us
  blocking collectives: 71.1 us -> 0 us
  starting transfers between devices: 0.52 us -> 60.1 us
  local copies, waits for them, and re-layouts: 77.2 us -> 39.1 us
  matrix products: 53.9 us -> 18.4 us
  Pallas kernels: 0 us -> 17.2 us
    reduce_scatter x5 -> x0, waiting for transfers between devices: 343 us -> none  [the longest x1 80.5 us: body(): lax.psum_scatter(grad_up * grad_scale, 'fsdp', scatter_dimension=0, tiled...]
    ppermute x0 -> x64, waiting for transfers between devices: none -> 168 us  [swap(): return lax.ppermute(value, axis, [(i, i ^ mask) for i in range(count)])]
    all_gather x6 -> x0, waiting for transfers between devices: 161 us -> none  [the longest x1 42.8 us: body(): lax.all_gather(keys_own, 'seq', axis=1, tiled=True)]
    psum x1, waiting for transfers between devices: 179 us -> 28.3 us  [body(): lax.psum((grad_down, grad_up_rows, grad_out), 'seq')]
    ppermute x0 -> x64, starting transfers between devices: none -> 60.1 us  [swap(): return lax.ppermute(value, axis, [(i, i ^ mask) for i in range(count)])]
    unnamed x14 -> x1, waiting for transfers between devices: 50.2 us -> 0.02 us
    unnamed x108 -> x88, local copies, waits for them, and re-layouts: 45.6 us -> 2.26 us
    psum x1 -> x0, blocking collectives: 39.5 us -> none  [body(): lax.psum((share_qkv, share_bq, share_bv, share_out, share_bout, share_gon...]
  transfers between devices with their start and end apart: 13 -> 65, of which waited for: 12 -> 34; matrix products, arithmetic and copies ran while one was open for 8% -> 12% of each run, Pallas kernels for 0% -> 3%
where the time goes in v1:
time: 374 us; the launch traced here: 373 us
  waiting for transfers between devices  196 us (52%)
  starting transfers between devices  60.1 us (16%)
  local copies, waits for them, and re-layouts  39.1 us (10%)
  other arithmetic  25.6 us (7%)
  matrix products  18.4 us (5%)
  Pallas kernels  17.2 us (5%)
  between operations  16.6 us (4%)
    ppermute x64, waiting for transfers between devices, swap(): return lax.ppermute(value, axis, [(i, i ^ mask) for i in range(count)])  168 us
    ppermute x64, starting transfers between devices, swap(): return lax.ppermute(value, axis, [(i, i ^ mask) for i in range(count)])  60.1 us
    psum x1, waiting for transfers between devices, body(): lax.psum((grad_down, grad_up_rows, grad_out), 'seq')  28.3 us
    convert_element_type x4, local copies, waits for them, and re-layouts, body(): sum_qkv.astype(f32)  11.3 us
    pallas_call x1, Pallas kernels, attend_back(): pl.pallas_call(functools.partial(attend_back_kernel, heads, size, size **...  10.1 us
    dot_general x4, matrix products, dot_tn(): lax.dot_general(a, b, (((0,), (0,)), ((), ())), preferred_element_type=f32)  7.56 us
  transfers between devices with their start and end apart: 65, of which 34 were waited for; matrix products, arithmetic and copies ran while one was open for 12% of the time, Pallas kernels for 3%

profile of v1, /device:TPU:0, one launch (start us, length us, event | category | flops | bytes accessed | tf_op | source)
XLA Modules:
  0.0 373.3 jit_solution(15912764385476799299)
XLA Ops:
  12.0 3.0 collective-permute-start.12
  15.0 2.9 reshape.245
  26.1 13.3 %collective-permute-done = bf16[128,768]{1,0:T(8,128)(2,1)S(1)} collective-permute-done((bf16[128,768]{1,0:T(8,128)(2,1)S(1)}, bf16[128,768]{1,0:T(8,128)(2,1)S(1)}, u32[]{:S(2)}, u32[]{:S(2)}) %collective-permute-start) | collective-permute-done | bytes 196640 | tf_op jit(solution)/shard_map/ppermute | solution.py:48
  42.3 2.5 fusion.5
  44.8 1.4 copy.96
  46.3 3.7 collective-permute-start.7
  50.8 1.6 collective-permute-start.8
  52.4 8.4 %collective-permute-done.5 = bf16[128,576]{1,0:T(8,128)(2,1)S(1)} collective-permute-done((bf16[128,576]{1,0:T(8,128)(2,1)S(1)}, bf16[128,576]{1,0:T(8,128)(2,1)S(1)}, u32[]{:S(2)}, u32[]{:S(2)}) %collective-permute-start.5) | collective-permute-done | bytes 147488 | tf_op jit(solution)/shard_map/ppermute | solution.py:48
  61.0 1.6 collective-permute-start.9
  62.6 1.6 collective-permute-done.6
  64.3 1.6 collective-permute-start.10
  67.4 2.4 collective-permute-done.10
  72.1 7.1 %attend.1 = (bf16[512,192]{1,0:T(8,128)(2,1)}, f32[512,128]{1,0:T(8,128)}) custom-call(bf16[512,192]{1,0:T(8,128)(2,1)} %pad_maximum_fusion.25.q_ref, bf16[1024,192]{1,0:T(8,128)(2,1)} %get-tuple-element.81.k_ref, bf16[1024,192]{1,0:T(8,128)(2,1)} %get-tuple-element.80.v_ref, f32[1,1024]{1,0:T(1,128)} %bitcast.256), custom_call_target="tpu_custom_call" | custom-call | flops 402653184 | bytes 1179648 | tf_op jit(solution)/shard_map/attend/pallas_call | solution.py:125
  80.2 2.5 collective-permute-start.16
  83.0 1.7 collective-permute-start.14
  84.7 2.0 collective-permute-done.16
  86.7 1.7 collective-permute-done.15
  88.6 1.5 fusion.73
  91.4 2.9 reshape.250
  97.7 5.4 %collective-permute-done.18 = bf16[128,768]{1,0:T(8,128)(2,1)} collective-permute-done((bf16[128,768]{1,0:T(8,128)(2,1)S(1)}, bf16[128,768]{1,0:T(8,128)(2,1)}, u32[]{:S(2)}, u32[]{:S(2)}) %collective-permute-start.18) | collective-permute-done | bytes 196640 | tf_op jit(solution)/shard_map/ppermute | solution.py:48
  105.9 2.4 constant_dynamic-slice_fusion.25
  111.3 6.4 %collective-permute-done.23 = bf16[192,768]{1,0:T(8,128)(2,1)S(1)} collective-permute-done((bf16[192,768]{1,0:T(8,128)(2,1)S(1)}, bf16[192,768]{1,0:T(8,128)(2,1)S(1)}, u32[]{:S(2)}, u32[]{:S(2)}) %collective-permute-start.23) | collective-permute-done | bytes 294944 | tf_op jit(solution)/shard_map/ppermute | solution.py:48
  117.7 6.0 %collective-permute-done.22 = bf16[192,768]{1,0:T(8,128)(2,1)S(1)} collective-permute-done((bf16[192,768]{1,0:T(8,128)(2,1)S(1)}, bf16[192,768]{1,0:T(8,128)(2,1)S(1)}, u32[]{:S(2)}, u32[]{:S(2)}) %collective-permute-start.22) | collective-permute-done | bytes 294944 | tf_op jit(solution)/shard_map/ppermute | solution.py:48
  124.1 2.0 multiply_convert_fusion.3
  127.3 1.6 collective-permute-done.24
  130.5 5.5 %collective-permute-done.25 = bf16[128,768]{1,0:T(8,128)(2,1)S(1)} collective-permute-done((bf16[128,768]{1,0:T(8,128)(2,1)S(1)}, bf16[128,768]{1,0:T(8,128)(2,1)S(1)}, u32[]{:S(2)}, u32[]{:S(2)}) %collective-permute-start.25) | collective-permute-done | bytes 196640 | tf_op jit(solution)/shard_map/ppermute | solution.py:48
  138.9 4.9 %collective-permute-done.26 = bf16[128,768]{1,0:T(8,128)(2,1)S(1)} collective-permute-done((bf16[128,768]{1,0:T(8,128)(2,1)S(1)}, bf16[128,768]{1,0:T(8,128)(2,1)S(1)}, u32[]{:S(2)}, u32[]{:S(2)}) %collective-permute-start.26) | collective-permute-done | bytes 196640 | tf_op jit(solution)/shard_map/ppermute | solution.py:48
  143.9 1.7 collective-permute-done.27
  145.6 1.9 fusion.72
  148.7 1.6 collective-permute-done.28
  151.7 1.6 collective-permute-start.61
  153.3 4.1 %collective-permute-done.29 = bf16[128,768]{1,0:T(8,128)(2,1)S(1)} collective-permute-done((bf16[128,768]{1,0:T(8,128)(2,1)S(1)}, bf16[128,768]{1,0:T(8,128)(2,1)S(1)}, u32[]{:S(2)}, u32[]{:S(2)}) %collective-permute-start.29) | collective-permute-done | bytes 196640 | tf_op jit(solution)/shard_map/ppermute | solution.py:48
  160.1 2.1 multiply_convert_fusion.1
  162.2 2.4 collective-permute-done.53
  167.4 2.1 collective-permute-start.55
  169.5 1.9 multiply_convert_fusion
  175.1 2.0 collective-permute-start.34
  177.5 2.0 collective-permute-start.32
  181.7 2.0 collective-permute-done.33
  185.3 10.1 %attend_back.1 = (f32[512,192]{1,0:T(8,128)}, f32[1024,192]{1,0:T(8,128)}, f32[1024,192]{1,0:T(8,128)}) custom-call(bf16[512,192]{1,0:T(8,128)(2,1)} %pad_maximum_fusion.25.q_ref, bf16[1024,192]{1,0:T(8,128)(2,1)} %get-tuple-element.81.k_ref, bf16[1024,192]{1,0:T(8,128)(2,1)} %get-tuple-element.80.v_ref, f32[1,1024]{1,0:T(1,128)} %bitcast.257, ...), custom_call_target="tpu_custom_call" | custom-call | flops 1006632960 | bytes 2359296 | tf_op jit(solution)/shard_map/attend_back/pallas_call | solution.py:198
  200.1 6.9 %collective-permute-done.35 = bf16[512,384]{1,0:T(8,128)(2,1)S(1)} collective-permute-done((bf16[512,384]{1,0:T(8,128)(2,1)S(1)}, bf16[512,384]{1,0:T(8,128)(2,1)S(1)}, u32[]{:S(2)}, u32[]{:S(2)}) %collective-permute-start.35) | collective-permute-done | bytes 393248 | tf_op jit(solution)/shard_map/ppermute | solution.py:48
  207.6 1.6 collective-permute-start.38
  210.0 2.0 collective-permute-start.36
  212.6 3.9 %collective-permute-done.38 = bf16[128,576]{1,0:T(8,128)(2,1)S(1)} collective-permute-done((bf16[128,576]{1,0:T(8,128)(2,1)S(1)}, bf16[128,576]{1,0:T(8,128)(2,1)S(1)}, u32[]{:S(2)}, u32[]{:S(2)}) %collective-permute-start.38) | collective-permute-done | bytes 147488 | tf_op jit(solution)/shard_map/ppermute | solution.py:48
  216.5 7.5 %collective-permute-done.37 = bf16[128,576]{1,0:T(8,128)(2,1)S(1)} collective-permute-done((bf16[128,576]{1,0:T(8,128)(2,1)S(1)}, bf16[128,576]{1,0:T(8,128)(2,1)S(1)}, u32[]{:S(2)}, u32[]{:S(2)}) %collective-permute-start.37) | collective-permute-done | bytes 147488 | tf_op jit(solution)/shard_map/ppermute | solution.py:48
  225.1 2.6 multiply_convert_fusion.2
  227.7 1.8 copy.87
  232.2 16.9 %collective-permute-done.41 = bf16[4,4,24,576]{3,2,1,0:T(8,128)(2,1)S(1)} collective-permute-done((bf16[4,4,24,576]{3,2,1,0:T(8,128)(2,1)S(1)}, bf16[4,4,24,576]{3,2,1,0:T(8,128)(2,1)S(1)}, u32[]{:S(2)}, u32[]{:S(2)}) %collective-permute-start.41) | collective-permute-done | bytes 442400 | tf_op jit(solution)/shard_map/ppermute | solution.py:48
  249.4 2.1 collective-permute-start.51
  251.5 17.4 %collective-permute-done.42 = bf16[2,4,24,576]{3,2,1,0:T(8,128)(2,1)S(1)} collective-permute-done((bf16[2,4,24,576]{3,2,1,0:T(8,128)(2,1)S(1)}, bf16[2,4,24,576]{3,2,1,0:T(8,128)(2,1)S(1)}, u32[]{:S(2)}, u32[]{:S(2)}) %collective-permute-start.42) | collective-permute-done | bytes 221216 | tf_op jit(solution)/shard_map/ppermute | solution.py:48
  269.1 1.6 collective-permute-start.52
  270.7 6.0 %collective-permute-done.43 = bf16[1,4,24,576]{3,2,1,0:T(8,128)(2,1)S(1)} collective-permute-done((bf16[1,4,24,576]{3,2,1,0:T(8,128)(2,1)S(1)}, bf16[1,4,24,576]{3,2,1,0:T(8,128)(2,1)S(1)}, u32[]{:S(2)}, u32[]{:S(2)}) %collective-permute-start.43) | collective-permute-done | bytes 110624 | tf_op jit(solution)/shard_map/ppermute | solution.py:48
  281.1 13.8 %collective-permute-done.47 = bf16[1,1,4,24,576]{4,3,2,1,0:T(8,128)(2,1)S(1)} collective-permute-done((bf16[1,1,4,24,576]{4,3,2,1,0:T(8,128)(2,1)S(1)}, bf16[1,1,4,24,576]{4,3,2,1,0:T(8,128)(2,1)S(1)}, u32[]{:S(2)}, u32[]{:S(2)}) %collective-permute-start.47) | collective-permute-done | bytes 110624 | tf_op jit(solution)/shard_map/ppermute | solution.py:48
  296.5 6.2 %collective-permute-done.48 = bf16[2,1,4,24,576]{4,3,2,0,1:T(8,128)(2,1)S(1)} collective-permute-done((bf16[2,1,4,24,576]{4,3,2,0,1:T(8,128)(2,1)S(1)}, bf16[2,1,4,24,576]{4,3,2,0,1:T(8,128)(2,1)S(1)}, u32[]{:S(2)}, u32[]{:S(2)}) %collective-permute-start.48) | collective-permute-done | bytes 221216 | tf_op jit(solution)/shard_map/ppermute | solution.py:48
  302.9 1.5 collective-permute-start.49
  305.8 14.0 %collective-permute-done.49 = bf16[4,1,4,24,576]{4,3,2,0,1:T(8,128)(2,1)S(1)} collective-permute-done((bf16[4,1,4,24,576]{4,3,2,0,1:T(8,128)(2,1)S(1)}, bf16[4,1,4,24,576]{4,3,2,0,1:T(8,128)(2,1)S(1)}, u32[]{:S(2)}, u32[]{:S(2)}) %collective-permute-start.49) | collective-permute-done | bytes 442400 | tf_op jit(solution)/shard_map/ppermute | solution.py:48
  320.1 1.4 copy.93
  321.5 3.3 reshape.272
  324.8 2.9 copy.94
  327.7 3.8 %reshape.270 = f32[192,2304]{1,0:T(8,128)} reshape(f32[8,24,3,4,192]{4,3,2,1,0:T(4,128)} %copy.94) | data formatting | bytes 3538944 | tf_op jit(solution)/shard_map/convert_element_type | solution.py:437
  331.5 28.3 %all-reduce.3.cloned.1.call-done = (bf16[192,768]{1,0:T(8,128)(2,1)}, bf16[4,192,768]{2,1,0:T(8,128)(2,1)}, bf16[768,768]{1,0:T(8,128)(2,1)}) async-done(((bf16[192,768]{1,0:T(8,128)(2,1)}, bf16[4,192,768]{2,1,0:T(8,128)(2,1)}, bf16[768,768]{1,0:T(8,128)(2,1)}), (bf16[192,768]{1,0:T(8,128)(2,1)}, bf16[4,192,768]{2,1,0:T(8,128)(2,1)}, bf16[768,768]{1,0:T(8,128)(2,1)})) %all-reduce.3.cloned.1.call-update) | async-done | bytes 2654224 | tf_op jit(solution)/shard_map/psum | solution.py:390
  359.8 1.8 convert_element_type.214
  363.1 1.7 copy.106
  364.8 1.6 convert_element_type.220
  (325 shorter events, 72.9 us)
Async XLA Ops:
  7.2 352.6 %all-reduce.3.cloned.1.call-start = ((), (), s32[]{:S(2)}) async-start(), calls=%async_computation | async-start | bytes 5308416 | tf_op jit(solution)/shard_map/psum | solution.py:390
  12.0 10.4 %collective-permute-start.12 = (f32[1,7,192]{2,1,0:T(8,128)S(1)}, f32[1,7,192]{2,1,0:T(8,128)S(1)}, u32[]{:S(2)}, u32[]{:S(2)}) collective-permute-start(f32[1,7,192]{2,1,0:T(8,128)S(1)} %bitcast.240), channel_id=1, source_target_pairs={{0,2},{1,3},{2,0},{3,1},{4,6},{5,7},{6,4},{7,5},{8,10},{9,11},{10,... | collective-permute-start | bytes 16136 | tf_op jit(solution)/shard_map/ppermute | solution.py:48
  19.9 20.4 %collective-permute-start.4 = (bf16[192,576]{0,1:T(8,128)(2,1)}, bf16[192,576]{0,1:T(8,128)(2,1)S(1)}, u32[]{:S(2)}, u32[]{:S(2)}) collective-permute-start(bf16[192,576]{0,1:T(8,128)(2,1)} %get-tuple-element.65), channel_id=1, source_target_pairs={{0,3},{1,2},{2,1},{3,0},{4,7},{5,6},{6,5},{7,4},{8,11},{9,10},{10,... | collective-permute-start | bytes 663560 | tf_op jit(solution)/shard_map/ppermute | solution.py:48
  19.9 20.4 %collective-permute-start.3 = (bf16[192,576]{0,1:T(8,128)(2,1)}, bf16[192,576]{0,1:T(8,128)(2,1)S(1)}, u32[]{:S(2)}, u32[]{:S(2)}) collective-permute-start(bf16[192,576]{0,1:T(8,128)(2,1)} %get-tuple-element.66), channel_id=1, source_target_pairs={{0,2},{1,3},{2,0},{3,1},{4,6},{5,7},{6,4},{7,5},{8,10},{9,11},{10,... | collective-permute-start | bytes 663560 | tf_op jit(solution)/shard_map/ppermute | solution.py:48
  21.1 19.3 %collective-permute-start.2 = (bf16[192,576]{0,1:T(8,128)(2,1)}, bf16[192,576]{0,1:T(8,128)(2,1)S(1)}, u32[]{:S(2)}, u32[]{:S(2)}) collective-permute-start(bf16[192,576]{0,1:T(8,128)(2,1)} %get-tuple-element.67), channel_id=1, source_target_pairs={{0,1},{1,0},{2,3},{3,2},{4,5},{5,4},{6,7},{7,6},{8,9},{9,8},{10,11... | collective-permute-start | bytes 663560 | tf_op jit(solution)/shard_map/ppermute | solution.py:48
  21.8 17.7 %collective-permute-start = (bf16[128,768]{1,0:T(8,128)(2,1)S(1)}, bf16[128,768]{1,0:T(8,128)(2,1)S(1)}, u32[]{:S(2)}, u32[]{:S(2)}) collective-permute-start(bf16[128,768]{1,0:T(8,128)(2,1)S(1)} %bitcast.220), channel_id=1, source_target_pairs={{0,2},{1,3},{2,0},{3,1},{4,6},{5,7},{6,4},{7,5},{8,10},{9,11},{10,... | collective-permute-start | bytes 589832 | tf_op jit(solution)/shard_map/ppermute | solution.py:48
  40.2 2.1 collective-permute-start.1
  46.3 19.6 %collective-permute-start.7 = (bf16[128,576]{1,0:T(8,128)(2,1)S(1)}, bf16[128,576]{1,0:T(8,128)(2,1)S(1)}, u32[]{:S(2)}, u32[]{:S(2)}) collective-permute-start(bf16[128,576]{1,0:T(8,128)(2,1)S(1)} %get-tuple-element.91), channel_id=1, source_target_pairs={{0,24},{4,28},{8,16},{12,20},{16,8},{20,12},{24,0},{28,4},{1,25},{... | collective-permute-start | bytes 442376 | tf_op jit(solution)/shard_map/ppermute | solution.py:48
  49.9 14.2 %collective-permute-start.6 = (bf16[128,576]{1,0:T(8,128)(2,1)S(1)}, bf16[128,576]{1,0:T(8,128)(2,1)S(1)}, u32[]{:S(2)}, u32[]{:S(2)}) collective-permute-start(bf16[128,576]{1,0:T(8,128)(2,1)S(1)} %get-tuple-element.92), channel_id=1, source_target_pairs={{0,16},{4,20},{8,24},{12,28},{16,0},{20,4},{24,8},{28,12},{1,17},{... | collective-permute-start | bytes 442376 | tf_op jit(solution)/shard_map/ppermute | solution.py:48
  49.9 10.9 %collective-permute-start.5 = (bf16[128,576]{1,0:T(8,128)(2,1)S(1)}, bf16[128,576]{1,0:T(8,128)(2,1)S(1)}, u32[]{:S(2)}, u32[]{:S(2)}) collective-permute-start(bf16[128,576]{1,0:T(8,128)(2,1)S(1)} %get-tuple-element.93), channel_id=1, source_target_pairs={{0,8},{4,12},{8,0},{12,4},{16,24},{20,28},{24,16},{28,20},{1,9},{5... | collective-permute-start | bytes 442376 | tf_op jit(solution)/shard_map/ppermute | solution.py:48
  50.8 16.5 %collective-permute-start.8 = (bf16[128,384]{1,0:T(8,128)(2,1)S(1)}, bf16[128,384]{1,0:T(8,128)(2,1)S(1)}, u32[]{:S(2)}, u32[]{:S(2)}) collective-permute-start(bf16[128,384]{1,0:T(8,128)(2,1)S(1)} %get-tuple-element.119), channel_id=1, source_target_pairs={{0,4},{4,0},{8,12},{12,8},{16,20},{20,16},{24,28},{28,24},{1,5},{5... | collective-permute-start | bytes 294920 | tf_op jit(solution)/shard_map/ppermute | solution.py:48
  61.0 6.4 %collective-permute-start.9 = (bf16[128,384]{1,0:T(8,128)(2,1)S(1)}, bf16[128,384]{1,0:T(8,128)(2,1)S(1)}, u32[]{:S(2)}, u32[]{:S(2)}) collective-permute-start(bf16[128,384]{1,0:T(8,128)(2,1)S(1)} %get-tuple-element.117), channel_id=1, source_target_pairs={{0,4},{4,0},{8,12},{12,8},{16,20},{20,16},{24,28},{28,24},{1,5},{5... | collective-permute-start | bytes 294920 | tf_op jit(solution)/shard_map/ppermute | solution.py:48
  64.3 5.5 %collective-permute-start.10 = (bf16[128,384]{1,0:T(8,128)(2,1)S(1)}, bf16[128,384]{1,0:T(8,128)(2,1)S(1)}, u32[]{:S(2)}, u32[]{:S(2)}) collective-permute-start(bf16[128,384]{1,0:T(8,128)(2,1)S(1)} %get-tuple-element.115), channel_id=1, source_target_pairs={{0,4},{4,0},{8,12},{12,8},{16,20},{20,16},{24,28},{28,24},{1,5},{5... | collective-permute-start | bytes 294920 | tf_op jit(solution)/shard_map/ppermute | solution.py:48
  66.0 4.9 %collective-permute-start.11 = (bf16[128,384]{1,0:T(8,128)(2,1)S(1)}, bf16[128,384]{1,0:T(8,128)(2,1)S(1)}, u32[]{:S(2)}, u32[]{:S(2)}) collective-permute-start(bf16[128,384]{1,0:T(8,128)(2,1)S(1)} %get-tuple-element.113), channel_id=1, source_target_pairs={{0,4},{4,0},{8,12},{12,8},{16,20},{20,16},{24,28},{28,24},{1,5},{5... | collective-permute-start | bytes 294920 | tf_op jit(solution)/shard_map/ppermute | solution.py:48
  80.2 6.5 %collective-permute-start.16 = (bf16[128,192]{1,0:T(8,128)(2,1)S(1)}, bf16[128,192]{1,0:T(8,128)(2,1)S(1)}, u32[]{:S(2)}, u32[]{:S(2)}) collective-permute-start(bf16[128,192]{1,0:T(8,128)(2,1)S(1)} %get-tuple-element.108), channel_id=1, source_target_pairs={{0,24},{4,28},{8,16},{12,20},{16,8},{20,12},{24,0},{28,4},{1,25},{... | collective-permute-start | bytes 147464 | tf_op jit(solution)/shard_map/ppermute | solution.py:48
  82.7 5.7 %collective-permute-start.15 = (bf16[128,192]{1,0:T(8,128)(2,1)S(1)}, bf16[128,192]{1,0:T(8,128)(2,1)S(1)}, u32[]{:S(2)}, u32[]{:S(2)}) collective-permute-start(bf16[128,192]{1,0:T(8,128)(2,1)S(1)} %get-tuple-element.109), channel_id=1, source_target_pairs={{0,16},{4,20},{8,24},{12,28},{16,0},{20,4},{24,8},{28,12},{1,17},{... | collective-permute-start | bytes 147464 | tf_op jit(solution)/shard_map/ppermute | solution.py:48
  83.0 5.4 %collective-permute-start.14 = (bf16[128,192]{1,0:T(8,128)(2,1)S(1)}, bf16[128,192]{1,0:T(8,128)(2,1)S(1)}, u32[]{:S(2)}, u32[]{:S(2)}) collective-permute-start(bf16[128,192]{1,0:T(8,128)(2,1)S(1)} %get-tuple-element.110), channel_id=1, source_target_pairs={{0,8},{4,12},{8,0},{12,4},{16,24},{20,28},{24,16},{28,20},{1,9},{5... | collective-permute-start | bytes 147464 | tf_op jit(solution)/shard_map/ppermute | solution.py:48
  91.3 3.0 collective-permute-start.17
  95.7 7.5 %collective-permute-start.18 = (bf16[128,768]{1,0:T(8,128)(2,1)S(1)}, bf16[128,768]{1,0:T(8,128)(2,1)}, u32[]{:S(2)}, u32[]{:S(2)}) collective-permute-start(bf16[128,768]{1,0:T(8,128)(2,1)S(1)} %slice.374), channel_id=1, source_target_pairs={{0,2},{1,3},{2,0},{3,1},{4,6},{5,7},{6,4},{7,5},{8,10},{9,11},{10,... | collective-permute-start | bytes 589832 | tf_op jit(solution)/shard_map/ppermute | solution.py:48
  104.7 6.5 %collective-permute-start.19 = (bf16[128,768]{1,0:T(8,128)(2,1)S(1)}, bf16[128,768]{1,0:T(8,128)(2,1)S(1)}, u32[]{:S(2)}, u32[]{:S(2)}) collective-permute-start(bf16[128,768]{1,0:T(8,128)(2,1)S(1)} %fusion.31), channel_id=1, source_target_pairs={{0,2},{1,3},{2,0},{3,1},{4,6},{5,7},{6,4},{7,5},{8,10},{9,11},{10,... | collective-permute-start | bytes 589832 | tf_op jit(solution)/shard_map/ppermute | solution.py:48
  108.3 9.4 %collective-permute-start.23 = (bf16[192,768]{1,0:T(8,128)(2,1)S(1)}, bf16[192,768]{1,0:T(8,128)(2,1)S(1)}, u32[]{:S(2)}, u32[]{:S(2)}) collective-permute-start(bf16[192,768]{1,0:T(8,128)(2,1)S(1)} %bitcast.234), channel_id=1, source_target_pairs={{0,3},{1,2},{2,1},{3,0},{4,7},{5,6},{6,5},{7,4},{8,11},{9,10},{10,... | collective-permute-start | bytes 884744 | tf_op jit(solution)/shard_map/ppermute | solution.py:48
  108.5 15.2 %collective-permute-start.22 = (bf16[192,768]{1,0:T(8,128)(2,1)S(1)}, bf16[192,768]{1,0:T(8,128)(2,1)S(1)}, u32[]{:S(2)}, u32[]{:S(2)}) collective-permute-start(bf16[192,768]{1,0:T(8,128)(2,1)S(1)} %bitcast.235), channel_id=1, source_target_pairs={{0,2},{1,3},{2,0},{3,1},{4,6},{5,7},{6,4},{7,5},{8,10},{9,11},{10,... | collective-permute-start | bytes 884744 | tf_op jit(solution)/shard_map/ppermute | solution.py:48
  109.5 14.2 %collective-permute-start.21 = (bf16[192,768]{1,0:T(8,128)(2,1)S(1)}, bf16[192,768]{1,0:T(8,128)(2,1)S(1)}, u32[]{:S(2)}, u32[]{:S(2)}) collective-permute-start(bf16[192,768]{1,0:T(8,128)(2,1)S(1)} %bitcast.236), channel_id=1, source_target_pairs={{0,1},{1,0},{2,3},{3,2},{4,5},{5,4},{6,7},{7,6},{8,9},{9,8},{10,11... | collective-permute-start | bytes 884744 | tf_op jit(solution)/shard_map/ppermute | solution.py:48
  111.3 12.9 %collective-permute-start.20 = (bf16[256,768]{1,0:T(8,128)(2,1)S(1)}, bf16[256,768]{1,0:T(8,128)(2,1)S(1)}, u32[]{:S(2)}, u32[]{:S(2)}) collective-permute-start(bf16[256,768]{1,0:T(8,128)(2,1)S(1)} %pad_maximum_fusion.14), channel_id=1, source_target_pairs={{0,1},{1,0},{2,3},{3,2},{4,5},{5,4},{6,7},{7,6},{8,9},{9,8},{10,11... | collective-permute-start | bytes 1179656 | tf_op jit(solution)/shard_map/ppermute | solution.py:48
  127.1 1.8 collective-permute-start.24
  129.0 7.0 %collective-permute-start.25 = (bf16[128,768]{1,0:T(8,128)(2,1)S(1)}, bf16[128,768]{1,0:T(8,128)(2,1)S(1)}, u32[]{:S(2)}, u32[]{:S(2)}) collective-permute-start(bf16[128,768]{1,0:T(8,128)(2,1)S(1)} %slice.373), channel_id=1, source_target_pairs={{0,2},{1,3},{2,0},{3,1},{4,6},{5,7},{6,4},{7,5},{8,10},{9,11},{10,... | collective-permute-start | bytes 589832 | tf_op jit(solution)/shard_map/ppermute | solution.py:48
  137.7 6.2 %collective-permute-start.26 = (bf16[128,768]{1,0:T(8,128)(2,1)S(1)}, bf16[128,768]{1,0:T(8,128)(2,1)S(1)}, u32[]{:S(2)}, u32[]{:S(2)}) collective-permute-start(bf16[128,768]{1,0:T(8,128)(2,1)S(1)} %convert_element_type.188), channel_id=1, source_target_pairs={{0,2},{1,3},{2,0},{3,1},{4,6},{5,7},{6,4},{7,5},{8,10},{9,11},{10,... | collective-permute-start | bytes 589832 | tf_op jit(solution)/shard_map/ppermute | solution.py:48
  143.8 1.8 collective-permute-start.27
  148.5 1.8 collective-permute-start.28
  150.4 7.0 %collective-permute-start.29 = (bf16[128,768]{1,0:T(8,128)(2,1)S(1)}, bf16[128,768]{1,0:T(8,128)(2,1)S(1)}, u32[]{:S(2)}, u32[]{:S(2)}) collective-permute-start(bf16[128,768]{1,0:T(8,128)(2,1)S(1)} %slice.372), channel_id=1, source_target_pairs={{0,2},{1,3},{2,0},{3,1},{4,6},{5,7},{6,4},{7,5},{8,10},{9,11},{10,... | collective-permute-start | bytes 589832 | tf_op jit(solution)/shard_map/ppermute | solution.py:48
  151.7 15.2 %collective-permute-start.61 = (f32[768]{0:T(1024)S(1)}, f32[768]{0:T(1024)S(1)}, u32[]{:S(2)}, u32[]{:S(2)}) collective-permute-start(f32[768]{0:T(1024)S(1)} %get-tuple-element.146), channel_id=1, source_target_pairs={{0,16},{4,20},{8,24},{12,28},{16,0},{20,4},{24,8},{28,12},{1,17},{... | collective-permute-start | bytes 9224 | tf_op jit(solution)/shard_map/ppermute | solution.py:48
  157.9 6.8 %collective-permute-start.30 = (bf16[128,768]{1,0:T(8,128)(2,1)S(1)}, bf16[128,768]{1,0:T(8,128)(2,1)S(1)}, u32[]{:S(2)}, u32[]{:S(2)}) collective-permute-start(bf16[128,768]{1,0:T(8,128)(2,1)S(1)} %convert_element_type.192), channel_id=1, source_target_pairs={{0,2},{1,3},{2,0},{3,1},{4,6},{5,7},{6,4},{7,5},{8,10},{9,11},{10,... | collective-permute-start | bytes 589832 | tf_op jit(solution)/shard_map/ppermute | solution.py:48
  159.2 5.4 %collective-permute-start.53 = (f32[6,768]{1,0:T(8,128)S(1)}, f32[6,768]{1,0:T(8,128)S(1)}, u32[]{:S(2)}, u32[]{:S(2)}) collective-permute-start(f32[6,768]{1,0:T(8,128)S(1)} %stack.282), channel_id=1, source_target_pairs={{0,2},{1,3},{2,0},{3,1},{4,6},{5,7},{6,4},{7,5},{8,10},{9,11},{10,... | collective-permute-start | bytes 55304 | tf_op jit(solution)/shard_map/ppermute | solution.py:48
  164.6 2.8 collective-permute-start.54
  164.7 9.0 %collective-permute-start.31 = (bf16[256,768]{1,0:T(8,128)(2,1)S(1)}, bf16[256,768]{1,0:T(8,128)(2,1)S(1)}, u32[]{:S(2)}, u32[]{:S(2)}) collective-permute-start(bf16[256,768]{1,0:T(8,128)(2,1)S(1)} %pad_maximum_fusion.16), channel_id=1, source_target_pairs={{0,1},{1,0},{2,3},{3,2},{4,5},{5,4},{6,7},{7,6},{8,9},{9,8},{10,11... | collective-permute-start | bytes 1179656 | tf_op jit(solution)/shard_map/ppermute | solution.py:48
  166.1 31.9 %collective-permute-start.60 = (bf16[192,768]{1,0:T(8,128)(2,1)}, bf16[192,768]{1,0:T(8,128)(2,1)S(1)}, u32[]{:S(2)}, u32[]{:S(2)}) collective-permute-start(bf16[192,768]{1,0:T(8,128)(2,1)} %get-tuple-element.57), channel_id=1, source_target_pairs={{0,3},{1,2},{2,1},{3,0},{4,7},{5,6},{6,5},{7,4},{8,11},{9,10},{10,... | collective-permute-start | bytes 884744 | tf_op jit(solution)/shard_map/ppermute | solution.py:48
  166.9 4.5 %collective-permute-start.62 = (f32[768]{0:T(1024)S(1)}, f32[768]{0:T(1024)S(1)}, u32[]{:S(2)}, u32[]{:S(2)}) collective-permute-start(f32[768]{0:T(1024)S(1)} %add.390), channel_id=1, source_target_pairs={{0,8},{4,12},{8,0},{12,4},{16,24},{20,28},{24,16},{28,20},{1,9},{5... | collective-permute-start | bytes 9224 | tf_op jit(solution)/shard_map/ppermute | solution.py:48
  167.4 5.1 %collective-permute-start.55 = (f32[6,768]{1,0:T(8,128)S(1)}, f32[6,768]{1,0:T(8,128)S(1)}, u32[]{:S(2)}, u32[]{:S(2)}) collective-permute-start(f32[6,768]{1,0:T(8,128)S(1)} %add.385), channel_id=1, source_target_pairs={{0,16},{4,20},{8,24},{12,28},{16,0},{20,4},{24,8},{28,12},{1,17},{... | collective-permute-start | bytes 55304 | tf_op jit(solution)/shard_map/ppermute | solution.py:48
  171.4 6.1 %collective-permute-start.63 = (f32[768]{0:T(1024)S(1)}, f32[768]{0:T(1024)S(1)}, u32[]{:S(2)}, u32[]{:S(2)}) collective-permute-start(f32[768]{0:T(1024)S(1)} %add.391), channel_id=1, source_target_pairs={{0,4},{4,0},{8,12},{12,8},{16,20},{20,16},{24,28},{28,24},{1,5},{5... | collective-permute-start | bytes 9224 | tf_op jit(solution)/shard_map/ppermute | solution.py:48
  172.5 7.6 %collective-permute-start.56 = (f32[6,768]{1,0:T(8,128)S(1)}, f32[6,768]{1,0:T(8,128)S(1)}, u32[]{:S(2)}, u32[]{:S(2)}) collective-permute-start(f32[6,768]{1,0:T(8,128)S(1)} %add.386), channel_id=1, source_target_pairs={{0,8},{4,12},{8,0},{12,4},{16,24},{20,28},{24,16},{28,20},{1,9},{5... | collective-permute-start | bytes 55304 | tf_op jit(solution)/shard_map/ppermute | solution.py:48
  175.1 6.6 %collective-permute-start.34 = (bf16[128,192]{1,0:T(8,128)(2,1)S(1)}, bf16[128,192]{1,0:T(8,128)(2,1)S(1)}, u32[]{:S(2)}, u32[]{:S(2)}) collective-permute-start(bf16[128,192]{1,0:T(8,128)(2,1)S(1)} %get-tuple-element.100), channel_id=1, source_target_pairs={{0,24},{4,28},{8,16},{12,20},{16,8},{20,12},{24,0},{28,4},{1,25},{... | collective-permute-start | bytes 147464 | tf_op jit(solution)/shard_map/ppermute | solution.py:48
  177.1 6.6 %collective-permute-start.33 = (bf16[128,192]{1,0:T(8,128)(2,1)S(1)}, bf16[128,192]{1,0:T(8,128)(2,1)S(1)}, u32[]{:S(2)}, u32[]{:S(2)}) collective-permute-start(bf16[128,192]{1,0:T(8,128)(2,1)S(1)} %get-tuple-element.101), channel_id=1, source_target_pairs={{0,16},{4,20},{8,24},{12,28},{16,0},{20,4},{24,8},{28,12},{1,17},{... | collective-permute-start | bytes 147464 | tf_op jit(solution)/shard_map/ppermute | solution.py:48
  177.5 7.1 %collective-permute-start.32 = (bf16[128,192]{1,0:T(8,128)(2,1)S(1)}, bf16[128,192]{1,0:T(8,128)(2,1)S(1)}, u32[]{:S(2)}, u32[]{:S(2)}) collective-permute-start(bf16[128,192]{1,0:T(8,128)(2,1)S(1)} %get-tuple-element.102), channel_id=1, source_target_pairs={{0,8},{4,12},{8,0},{12,4},{16,24},{20,28},{24,16},{28,20},{1,9},{5... | collective-permute-start | bytes 147464 | tf_op jit(solution)/shard_map/ppermute | solution.py:48
  180.2 17.8 %collective-permute-start.59 = (bf16[192,768]{1,0:T(8,128)(2,1)S(1)}, bf16[192,768]{1,0:T(8,128)(2,1)S(1)}, u32[]{:S(2)}, u32[]{:S(2)}) collective-permute-start(bf16[192,768]{1,0:T(8,128)(2,1)S(1)} %get-tuple-element.58), channel_id=1, source_target_pairs={{0,2},{1,3},{2,0},{3,1},{4,6},{5,7},{6,4},{7,5},{8,10},{9,11},{10,... | collective-permute-start | bytes 884744 | tf_op jit(solution)/shard_map/ppermute | solution.py:48
  181.7 16.3 %collective-permute-start.58 = (bf16[192,768]{1,0:T(8,128)(2,1)S(1)}, bf16[192,768]{1,0:T(8,128)(2,1)S(1)}, u32[]{:S(2)}, u32[]{:S(2)}) collective-permute-start(bf16[192,768]{1,0:T(8,128)(2,1)S(1)} %get-tuple-element.59), channel_id=1, source_target_pairs={{0,1},{1,0},{2,3},{3,2},{4,5},{5,4},{6,7},{7,6},{8,9},{9,8},{10,11... | collective-permute-start | bytes 884744 | tf_op jit(solution)/shard_map/ppermute | solution.py:48
  183.7 15.5 %collective-permute-start.57 = (f32[6,768]{1,0:T(8,128)}, f32[6,768]{1,0:T(8,128)}, u32[]{:S(2)}, u32[]{:S(2)}) collective-permute-start(f32[6,768]{1,0:T(8,128)} %add.387), channel_id=1, source_target_pairs={{0,4},{4,0},{8,12},{12,8},{16,20},{20,16},{24,28},{28,24},{1,5},{5... | collective-permute-start | bytes 55304 | tf_op jit(solution)/shard_map/ppermute | solution.py:48
  196.8 10.2 %collective-permute-start.35 = (bf16[512,384]{1,0:T(8,128)(2,1)S(1)}, bf16[512,384]{1,0:T(8,128)(2,1)S(1)}, u32[]{:S(2)}, u32[]{:S(2)}) collective-permute-start(bf16[512,384]{1,0:T(8,128)(2,1)S(1)} %fusion.10), channel_id=1, source_target_pairs={{0,4},{4,0},{8,12},{12,8},{16,20},{20,16},{24,28},{28,24},{1,5},{5... | collective-permute-start | bytes 1179656 | tf_op jit(solution)/shard_map/ppermute | solution.py:48
  207.6 8.9 %collective-permute-start.38 = (bf16[128,576]{1,0:T(8,128)(2,1)S(1)}, bf16[128,576]{1,0:T(8,128)(2,1)S(1)}, u32[]{:S(2)}, u32[]{:S(2)}) collective-permute-start(bf16[128,576]{1,0:T(8,128)(2,1)S(1)} %get-tuple-element.88), channel_id=1, source_target_pairs={{0,24},{4,28},{8,16},{12,20},{16,8},{20,12},{24,0},{28,4},{1,25},{... | collective-permute-start | bytes 442376 | tf_op jit(solution)/shard_map/ppermute | solution.py:48
  209.1 14.9 %collective-permute-start.37 = (bf16[128,576]{1,0:T(8,128)(2,1)S(1)}, bf16[128,576]{1,0:T(8,128)(2,1)S(1)}, u32[]{:S(2)}, u32[]{:S(2)}) collective-permute-start(bf16[128,576]{1,0:T(8,128)(2,1)S(1)} %get-tuple-element.89), channel_id=1, source_target_pairs={{0,16},{4,20},{8,24},{12,28},{16,0},{20,4},{24,8},{28,12},{1,17},{... | collective-permute-start | bytes 442376 | tf_op jit(solution)/shard_map/ppermute | solution.py:48
  210.0 14.0 %collective-permute-start.36 = (bf16[128,576]{1,0:T(8,128)(2,1)S(1)}, bf16[128,576]{1,0:T(8,128)(2,1)S(1)}, u32[]{:S(2)}, u32[]{:S(2)}) collective-permute-start(bf16[128,576]{1,0:T(8,128)(2,1)S(1)} %get-tuple-element.87), channel_id=1, source_target_pairs={{0,8},{4,12},{8,0},{12,4},{16,24},{20,28},{24,16},{28,20},{1,9},{5... | collective-permute-start | bytes 442376 | tf_op jit(solution)/shard_map/ppermute | solution.py:48
  229.7 19.4 %collective-permute-start.41 = (bf16[4,4,24,576]{3,2,1,0:T(8,128)(2,1)S(1)}, bf16[4,4,24,576]{3,2,1,0:T(8,128)(2,1)S(1)}, u32[]{:S(2)}, u32[]{:S(2)}) collective-permute-start(bf16[4,4,24,576]{3,2,1,0:T(8,128)(2,1)S(1)} %bitcast.224), channel_id=1, source_target_pairs={{0,4},{4,0},{8,12},{12,8},{16,20},{20,16},{24,28},{28,24},{1,5},{5... | collective-permute-start | bytes 1327112 | tf_op jit(solution)/shard_map/ppermute | solution.py:48
  232.1 17.3 %collective-permute-start.50 = (f32[2,192]{1,0:T(2,128)S(1)}, f32[2,192]{1,0:T(2,128)S(1)}, u32[]{:S(2)}, u32[]{:S(2)}) collective-permute-start(f32[2,192]{1,0:T(2,128)S(1)} %pad_maximum_fusion.34), channel_id=1, source_target_pairs={{0,16},{4,20},{8,24},{12,28},{16,0},{20,4},{24,8},{28,12},{1,17},{... | collective-permute-start | bytes 4616 | tf_op jit(solution)/shard_map/ppermute | solution.py:48
  249.3 19.6 %collective-permute-start.42 = (bf16[2,4,24,576]{3,2,1,0:T(8,128)(2,1)S(1)}, bf16[2,4,24,576]{3,2,1,0:T(8,128)(2,1)S(1)}, u32[]{:S(2)}, u32[]{:S(2)}) collective-permute-start(bf16[2,4,24,576]{3,2,1,0:T(8,128)(2,1)S(1)} %dynamic-slice_bitcast_fusion.6), channel_id=1, source_target_pairs={{0,8},{4,12},{8,0},{12,4},{16,24},{20,28},{24,16},{28,20},{1,9},{5... | collective-permute-start | bytes 663560 | tf_op jit(solution)/shard_map/ppermute | solution.py:48
  249.4 19.7 %collective-permute-start.51 = (f32[2,192]{1,0:T(2,128)S(1)}, f32[2,192]{1,0:T(2,128)S(1)}, u32[]{:S(2)}, u32[]{:S(2)}) collective-permute-start(f32[2,192]{1,0:T(2,128)S(1)} %fusion.53), channel_id=1, source_target_pairs={{0,8},{4,12},{8,0},{12,4},{16,24},{20,28},{24,16},{28,20},{1,9},{5... | collective-permute-start | bytes 4616 | tf_op jit(solution)/shard_map/ppermute | solution.py:48
  269.0 7.7 %collective-permute-start.43 = (bf16[1,4,24,576]{3,2,1,0:T(8,128)(2,1)S(1)}, bf16[1,4,24,576]{3,2,1,0:T(8,128)(2,1)S(1)}, u32[]{:S(2)}, u32[]{:S(2)}) collective-permute-start(bf16[1,4,24,576]{3,2,1,0:T(8,128)(2,1)S(1)} %constant_dynamic-slice_fusion.11), channel_id=1, source_target_pairs={{0,16},{4,20},{8,24},{12,28},{16,0},{20,4},{24,8},{28,12},{1,17},{... | collective-permute-start | bytes 331784 | tf_op jit(solution)/shard_map/ppermute | solution.py:48
  269.1 12.0 %collective-permute-start.52 = (f32[2,192]{1,0:T(2,128)S(1)}, f32[2,192]{1,0:T(2,128)S(1)}, u32[]{:S(2)}, u32[]{:S(2)}) collective-permute-start(f32[2,192]{1,0:T(2,128)S(1)} %fusion.92), channel_id=1, source_target_pairs={{0,4},{4,0},{8,12},{12,8},{16,20},{20,16},{24,28},{28,24},{1,5},{5... | collective-permute-start | bytes 4616 | tf_op jit(solution)/shard_map/ppermute | solution.py:48
  276.8 3.4 collective-permute-start.46
  276.9 4.0 %collective-permute-start.45 = (bf16[24,576]{1,0:T(8,128)(2,1)S(1)}, bf16[24,576]{1,0:T(8,128)(2,1)S(1)}, u32[]{:S(2)}, u32[]{:S(2)}) collective-permute-start(bf16[24,576]{1,0:T(8,128)(2,1)S(1)} %get-tuple-element.127), channel_id=1, source_target_pairs={{0,2},{1,3},{2,0},{3,1},{4,6},{5,7},{6,4},{7,5},{8,10},{9,11},{10,... | collective-permute-start | bytes 82952 | tf_op jit(solution)/shard_map/ppermute | solution.py:48
  278.0 2.9 collective-permute-start.44
  279.6 15.5 %collective-permute-start.39 = (bf16[256,768]{1,0:T(8,128)(2,1)S(1)}, bf16[256,768]{1,0:T(8,128)(2,1)S(1)}, u32[]{:S(2)}, u32[]{:S(2)}) collective-permute-start(bf16[256,768]{1,0:T(8,128)(2,1)S(1)} %slice.367), channel_id=1, source_target_pairs={{0,1},{1,0},{2,3},{3,2},{4,5},{5,4},{6,7},{7,6},{8,9},{9,8},{10,11... | collective-permute-start | bytes 1179656 | tf_op jit(solution)/shard_map/ppermute | solution.py:48
  281.0 13.9 %collective-permute-start.47 = (bf16[1,1,4,24,576]{4,3,2,1,0:T(8,128)(2,1)S(1)}, bf16[1,1,4,24,576]{4,3,2,1,0:T(8,128)(2,1)S(1)}, u32[]{:S(2)}, u32[]{:S(2)}) collective-permute-start(bf16[1,1,4,24,576]{4,3,2,1,0:T(8,128)(2,1)S(1)} %maximum_bitcast_fusion.1), channel_id=1, source_target_pairs={{0,16},{4,20},{8,24},{12,28},{16,0},{20,4},{24,8},{28,12},{1,17},{... | collective-permute-start | bytes 331784 | tf_op jit(solution)/shard_map/ppermute | solution.py:48
  295.0 7.7 %collective-permute-start.48 = (bf16[2,1,4,24,576]{4,3,2,0,1:T(8,128)(2,1)S(1)}, bf16[2,1,4,24,576]{4,3,2,0,1:T(8,128)(2,1)S(1)}, u32[]{:S(2)}, u32[]{:S(2)}) collective-permute-start(bf16[2,1,4,24,576]{4,3,2,0,1:T(8,128)(2,1)S(1)} %maximum_bitcast_fusion), channel_id=1, source_target_pairs={{0,8},{4,12},{8,0},{12,4},{16,24},{20,28},{24,16},{28,20},{1,9},{5... | collective-permute-start | bytes 663560 | tf_op jit(solution)/shard_map/ppermute | solution.py:48
  295.2 9.8 %collective-permute-start.40 = (bf16[128,768]{1,0:T(8,128)(2,1)S(1)}, bf16[128,768]{1,0:T(8,128)(2,1)S(1)}, u32[]{:S(2)}, u32[]{:S(2)}) collective-permute-start(bf16[128,768]{1,0:T(8,128)(2,1)S(1)} %slice.371), channel_id=1, source_target_pairs={{0,2},{1,3},{2,0},{3,1},{4,6},{5,7},{6,4},{7,5},{8,10},{9,11},{10,... | collective-permute-start | bytes 589832 | tf_op jit(solution)/shard_map/ppermute | solution.py:48
  302.9 16.9 %collective-permute-start.49 = (bf16[4,1,4,24,576]{4,3,2,0,1:T(8,128)(2,1)S(1)}, bf16[4,1,4,24,576]{4,3,2,0,1:T(8,128)(2,1)S(1)}, u32[]{:S(2)}, u32[]{:S(2)}) collective-permute-start(bf16[4,1,4,24,576]{4,3,2,0,1:T(8,128)(2,1)S(1)} %bitcast.210), channel_id=1, source_target_pairs={{0,4},{4,0},{8,12},{12,8},{16,20},{20,16},{24,28},{28,24},{1,5},{5... | collective-permute-start | bytes 1327112 | tf_op jit(solution)/shard_map/ppermute | solution.py:48
  (41 other events, 296.7 us)
Sparse Core Ops, SparseCore 0:
  232.0 127.7 all-reduce.2
